TPU v7x, 512 devices: a whole 4x4x16 slice. The times are simulated.
512 devices in a mesh: dp: 16 (over x, y), heads: 16 (over z), side: 2 (over core).
Axes of the slice: x: 4, y: 4, z: 16, core: 2. Of those that a mesh axis runs over, the one named last changes fastest.
Arguments:
- queries: bfloat16 [384, 2, 4096], P('dp', None, ('heads', 'side')), may hold values from -6 to 6
- new_keys: bfloat16 [384, 2, 4096], P('dp', None, ('heads', 'side')), may hold values from -6 to 6
- new_values: bfloat16 [384, 2, 4096], P('dp', None, ('heads', 'side')), may hold values from -6 to 6
- head_states: bfloat16 [384, 32, 128, 128], P('dp', ('heads', 'side')), may hold values from -6 to 6
- slopes: float32 [32], P(('heads', 'side')), may hold values from 0.004 to 0.9
- head_gain: float32 [4096], P(('heads', 'side')), may hold values from 0.5 to 1.5
- out_weight: bfloat16 [4096, 3072], P(('heads', 'side')), may hold values from -0.1875 to 0.1875
- residual: bfloat16 [384, 2, 3072], P('dp', None, ('heads', 'side')), may hold values from -10 to 10
- norm_gain: float32 [3072], replicated, may hold values from 0.5 to 1.5
- expert_ids: int32 [384, 2, 2], P('dp'), may hold values from 0 to 15, all different within a row; in each aligned block of 48 rows (0 to 47, 48 to 95, ..., all dimensions but the last counted through in order) at most 9 rows name the same one
- expert_gates: float32 [384, 2, 2], P('dp'), may hold values from 0.2 to 1
- w_gate: bfloat16 [16, 16, 192, 4608], P('dp', None, 'side', 'heads'), may hold values from -0.109375 to 0.109375
- w_up: bfloat16 [16, 16, 192, 4608], P('dp', None, 'side', 'heads'), may hold values from -0.109375 to 0.109375
- w_down: bfloat16 [16, 4608, 16, 192], P('dp', 'heads', None, 'side'), may hold values from -0.125 to 0.125
Outputs:
- state_out: bfloat16 [384, 32, 128, 128], P('dp', ('heads', 'side'))
- resid_out: bfloat16 [384, 2, 3072], P('dp', None, ('heads', 'side'))
- moe_out: bfloat16 [384, 2, 3072], P('dp', None, ('heads', 'side'))
Inputs may be any that keep to these rules, and one draw needn't show every extreme that they name: `expert_ids`: among the 48 tokens of one dp index a token's 2 experts differ, no expert is chosen by more than 9 of them, and some expert is chosen by exactly 9.
All inputs are finite; a program needn't handle non-finite values.
Results may differ from a plain program's by a relative error of at most 0.025.
Values may be sent and summed in bfloat16 or wider, within the bound.
A program may use at most 64 MiB of HBM per device.

v0:
```python
import jax
import jax.numpy as jnp
from jax import lax
from jax.sharding import PartitionSpec as P


def local(
    queries,
    new_keys,
    new_values,
    head_states,
    slopes,
    head_gain,
    out_weight,
    residual,
    norm_gain,
    expert_ids,
    expert_gates,
    w_gate,
    w_up,
    w_down,
):
    requests_dev, step_count, inner_width = queries.shape
    local_heads = slopes.shape[0]
    head_size = inner_width // local_heads
    query_rows = queries.astype(jnp.float32).reshape(
        requests_dev, step_count, local_heads, head_size
    )
    key_rows = new_keys.astype(jnp.float32).reshape(
        requests_dev, step_count, local_heads, head_size
    )
    value_rows = new_values.astype(jnp.float32).reshape(
        requests_dev, step_count, local_heads, head_size
    )
    decays = jnp.exp(-slopes)[None, :, None, None]
    current = head_states.astype(jnp.float32)
    outputs = []
    for step in range(step_count):
        current = decays * current + key_rows[:, step, :, :, None] * value_rows[:, step, :, None, :]
        outputs.append(
            jnp.einsum(
                "rhi,rhij->rhj", query_rows[:, step], current, precision=lax.Precision.HIGHEST
            )
        )
    state_out = current.astype(jnp.bfloat16)
    head_output = jnp.stack(outputs, 1)
    scaled = head_output * lax.rsqrt(jnp.mean(head_output * head_output, -1, keepdims=True) + 1e-06)
    tokens_dev = requests_dev * step_count
    normed = (
        (scaled * head_gain.reshape(local_heads, head_size))
        .astype(jnp.bfloat16)
        .reshape(tokens_dev, inner_width)
    )
    partial_out = jnp.dot(normed, out_weight, preferred_element_type=jnp.float32)
    attention = lax.psum_scatter(partial_out, ("heads", "side"), scatter_dimension=1, tiled=True)
    width = norm_gain.shape[0]
    piece_width = attention.shape[1]
    resid_new = (residual.reshape(tokens_dev, piece_width).astype(jnp.float32) + attention).astype(
        jnp.bfloat16
    )
    stream = resid_new.astype(jnp.float32)
    sum_squares = lax.psum(jnp.sum(stream * stream, 1), ("heads", "side"))
    gain_piece = lax.dynamic_slice_in_dim(
        norm_gain, lax.axis_index(("heads", "side")) * piece_width, piece_width
    )
    mixed_in = (stream * lax.rsqrt(sum_squares / width + 1e-06)[:, None] * gain_piece).astype(
        jnp.bfloat16
    )
    groups = lax.axis_size("dp")
    heads_count = lax.axis_size("heads")
    choices_each = expert_ids.shape[2]
    capacity = max(2, 3 * choices_each * tokens_dev // (2 * groups))
    flat_ids = expert_ids.reshape(-1)
    onehot_table = (flat_ids[:, None] == jnp.arange(groups, dtype=jnp.int32)[None, :]).astype(
        jnp.int32
    )
    earlier = jnp.cumsum(onehot_table, 0) - onehot_table
    slot_index = jnp.sum(earlier * onehot_table, 1)
    target = flat_ids * capacity + slot_index
    source_row = jnp.arange(tokens_dev * choices_each, dtype=jnp.int32) // choices_each
    gate_flat = w_gate[0].reshape(-1, w_gate.shape[3])
    up_flat = w_up[0].reshape(-1, w_up.shape[3])
    down_flat = w_down[0].reshape(w_down.shape[1], -1)
    holder = jnp.zeros((groups * capacity, mixed_in.shape[1]), mixed_in.dtype)
    arrived = lax.all_to_all(
        holder.at[target].set(mixed_in[source_row]).reshape(groups, capacity, mixed_in.shape[1]),
        "dp",
        split_axis=0,
        concat_axis=0,
        tiled=True,
    )
    piece = lax.all_gather(arrived, "heads", axis=2, tiled=True)
    flat_piece = piece.reshape(-1, piece.shape[2])
    gate_part = jnp.dot(flat_piece, gate_flat, preferred_element_type=jnp.float32)
    up_part = jnp.dot(flat_piece, up_flat, preferred_element_type=jnp.float32)
    gate_val, up_val = (
        lax.psum(gate_part.astype(jnp.bfloat16), "side").astype(jnp.float32),
        lax.psum(up_part.astype(jnp.bfloat16), "side").astype(jnp.float32),
    )
    activation = (jax.nn.silu(gate_val) * up_val).astype(jnp.bfloat16)
    down_part = jnp.dot(activation, down_flat, preferred_element_type=jnp.float32).reshape(
        groups, capacity, heads_count, piece_width
    )
    reduced = lax.psum_scatter(
        down_part.astype(jnp.bfloat16), "heads", scatter_dimension=2, tiled=True
    )
    returned = lax.all_to_all(reduced, "dp", split_axis=0, concat_axis=0, tiled=True)
    picked = returned.reshape(groups * capacity, piece_width)[target].astype(jnp.float32)
    weighted = picked * expert_gates.reshape(-1)[:, None]
    moe_out = jnp.sum(weighted.reshape(tokens_dev, choices_each, piece_width), 1).astype(
        jnp.bfloat16
    )
    return (
        state_out,
        resid_new.reshape(requests_dev, step_count, piece_width),
        moe_out.reshape(requests_dev, step_count, piece_width),
    )


def solution(mesh):
    return jax.shard_map(
        local,
        mesh=mesh,
        in_specs=(
            P("dp", None, ("heads", "side")),
            P("dp", None, ("heads", "side")),
            P("dp", None, ("heads", "side")),
            P("dp", ("heads", "side"), None, None),
            P(("heads", "side")),
            P(("heads", "side")),
            P(("heads", "side"), None),
            P("dp", None, ("heads", "side")),
            P(),
            P("dp", None, None),
            P("dp", None, None),
            P("dp", None, "side", "heads"),
            P("dp", None, "side", "heads"),
            P("dp", "heads", None, "side"),
        ),
        out_specs=(
            P("dp", ("heads", "side"), None, None),
            P("dp", None, ("heads", "side")),
            P("dp", None, ("heads", "side")),
        ),
        check_vma=False,
    )
```

profile of v0, /device:TPU:8, one launch (start us, length us, event | category | flops | bytes accessed | tf_op | source)
XLA Modules:
  0.0 490.9 jit_solution(13953203980056573112)
XLA Ops:
  7.2 0.8 bitcast_convert_fusion.1
  8.1 0.7 bitcast_convert_fusion
  9.6 0.7 copy.73
  10.3 2.2 fusion.5
  12.5 1.8 fusion.8
  14.6 1.6 convolution_bitcast_fusion
  17.0 0.8 dynamic_slice.3
  17.9 113.7 %reduce-scatter.7.cloned.1.call-done = f32[96,48]{1,0:T(8,128)} async-done(((f32[3072,48]{1,0:T(8,128)}), f32[96,48]{1,0:T(8,128)}) %reduce-scatter.7.cloned.1.call-update) | async-done | bytes 18448
  131.6 0.9 copy.61
  132.6 45.8 %psum.21 = f32[48]{0:T(128)S(1)} all-reduce(f32[48]{0:T(128)S(1)} %get-tuple-element.5), channel_id=1, replica_groups=mesh['dp'=16,'heads'=16,'side'=2] {'heads','side'}, use_global_device_ids=true, to_apply=%region_5.6 | all-reduce | flops 48 | bytes 384 | tf_op jit(solution)/shard_map/psum | solution.py:62
  178.5 1.0 scatter_custom_fusion
  179.7 13.3 %all_to_all.10 = bf16[16,2,432]{2,1,0:T(2,128)(2,1)S(1)} all-to-all(bf16[16,2,432]{2,1,0:T(2,128)(2,1)S(1)} %reshape.300), channel_id=1, replica_groups=mesh['dp'=16,'heads'=16,'side'=2] {'dp'}, dimensions={0} | all-to-all | bytes 55296 | tf_op jit(solution)/shard_map/all_to_all | solution.py:85
  193.2 0.4 copy.44
  193.6 80.7 %all_gather.3 = bf16[16,9,1536]{1,0,2:T(8,128)(2,1)} all-gather(bf16[16,9,96]{1,0,2:T(8,128)(2,1)S(1)} %copy.44), channel_id=1, replica_groups=mesh['dp'=16,'heads'=16,'side'=2] {'heads'}, dimensions={2}, use_global_device_ids=true | all-gather | bytes 470016 | tf_op jit(solution)/shard_map/all_gather | solution.py:92
  274.2 8.2 %reshape.288 = bf16[144,1536]{0,1:T(8,128)(2,1)S(1)} reshape(bf16[16,9,1536]{1,0,2:T(8,128)(2,1)} %all_gather.3) | data formatting | bytes 884736 | tf_op jit(solution)/shard_map/reshape | solution.py:93
  282.5 1.1 convolution_convert_fusion.1
  283.6 0.2 copy-done.1
  283.8 1.1 convolution_convert_fusion.2
  284.9 2.4 reshape_squeeze.11
  287.3 0.7 copy.46
  288.0 36.9 %all-reduce.7.cloned.1.call-done = (bf16[144,288]{1,0:T(8,128)(2,1)}, bf16[144,288]{1,0:T(8,128)(2,1)}) async-done(((bf16[144,288]{1,0:T(8,128)(2,1)}, bf16[144,288]{1,0:T(8,128)(2,1)}), (bf16[144,288]{1,0:T(8,128)(2,1)}, bf16[144,288]{1,0:T(8,128)(2,1)})) %all-reduce.7.cloned.1.call-update) | async-done | bytes 165904 | tf_op jit(solution)/shard_map/psum | solution.py:98
  325.0 1.0 fusion.23
  326.0 1.6 convolution_convert_fusion
  327.7 1.3 dynamic-slice
  329.0 1.7 fusion.4
  330.7 136.5 %all-reduce.5.cloned.1.call-done = bf16[16,9,16,96]{3,0,2,1:T(8,128)(2,1)} async-done(((bf16[16,9,16,96]{3,0,2,1:T(8,128)(2,1)}), bf16[16,9,16,96]{3,0,2,1:T(8,128)(2,1)}) %all-reduce.5.cloned.1.call-update) | async-done | bytes 442384
  467.2 1.4 constant_dynamic-slice_fusion
  468.6 0.7 reshape.302
  469.3 7.3 %all-to-all-start.1 = ((bf16[16,2,432]{2,1,0:T(2,128)(2,1)}), bf16[16,2,432]{2,1,0:T(2,128)(2,1)S(1)}, u32[]{:S(2)}, u32[]{:S(2)}) async-start(bf16[16,2,432]{2,1,0:T(2,128)(2,1)} %reshape.302), calls=%async_computation.1 | async-start | bytes 65536 | tf_op jit(solution)/shard_map/all_to_all | solution.py:107
  476.7 6.1 %all-to-all-done.1 = bf16[16,2,432]{2,1,0:T(2,128)(2,1)S(1)} async-done(((bf16[16,2,432]{2,1,0:T(2,128)(2,1)}), bf16[16,2,432]{2,1,0:T(2,128)(2,1)S(1)}, u32[]{:S(2)}, u32[]{:S(2)}) %all-to-all-start.1) | async-done | bytes 27680 | tf_op jit(solution)/shard_map/all_to_all | solution.py:107
  483.0 0.7 gather_fusion
  483.7 0.7 fusion.25
  (54 shorter events, 2.2 us)
Async XLA Ops:
  7.2 275.3 %copy-start = (bf16[1,16,96,288]{3,2,1,0:T(8,128)(2,1)S(1)}, bf16[1,16,96,288]{3,2,1,0:T(8,128)(2,1)}, u32[]{:S(2)}) copy-start(bf16[1,16,96,288]{3,2,1,0:T(8,128)(2,1)} %param.26) | copy-start | bytes 2654212
  7.2 5.3 %copy-start.2 = (bf16[24,1,128,128]{3,2,1,0:T(8,128)(2,1)S(1)}, bf16[24,1,128,128]{3,2,1,0:T(8,128)(2,1)}, u32[]{:S(2)}) copy-start(bf16[24,1,128,128]{3,2,1,0:T(8,128)(2,1)} %param.17) | copy-start | bytes 2359300
  7.2 124.4 %reduce-scatter.7.cloned.1.call-start = ((), (), s32[]{:S(2)}) async-start(), calls=%async_computation.3 | async-start | bytes 1622016
  12.5 2.0 copy-start.4
  12.5 2.1 copy-start.9
  14.5 1.7 copy-start.7
  16.2 116.3 %copy-start.6 = (bf16[24,2,96]{2,1,0:T(2,128)(2,1)S(1)}, bf16[24,2,96]{2,1,0:T(2,128)(2,1)}, u32[]{:S(2)}) copy-start(bf16[24,2,96]{2,1,0:T(2,128)(2,1)} %param.21) | copy-start | bytes 27652
  16.2 308.8 %all-reduce.7.cloned.1.call-start = ((), (), s32[]{:S(2)}) async-start(), calls=%async_computation.5 | async-start | bytes 442368 | tf_op jit(solution)/shard_map/psum | solution.py:98
  132.6 141.6 %copy-start.5 = (bf16[48,96]{1,0:T(8,128)(2,1)}, bf16[48,96]{1,0:T(8,128)(2,1)S(1)}, u32[]{:S(2)}) copy-start(bf16[48,96]{1,0:T(8,128)(2,1)S(1)} %get-tuple-element.6) | copy-start | bytes 27652
  282.5 1.3 copy-start.1
  284.9 182.3 %all-reduce.5.cloned.1.call-start = ((), (), s32[]{:S(2)}) async-start(), calls=%async_computation.4 | async-start | bytes 1179648
  288.0 41.0 %copy-start.3 = (bf16[24,1,128,128]{3,2,1,0:T(8,128)(2,1)S(1)}, bf16[24,1,128,128]{3,2,1,0:T(8,128)(2,1)}, u32[]{:S(2)}) copy-start(bf16[24,1,128,128]{3,2,1,0:T(8,128)(2,1)} %param.17) | copy-start | bytes 2359300
  327.6 149.0 %copy-start.8 = (f32[24,2,2]{0,2,1:T(2,128)S(1)}, f32[24,2,2]{0,2,1:T(2,128)}, u32[]{:S(2)}) copy-start(f32[24,2,2]{0,2,1:T(2,128)} %param.24) | copy-start | bytes 1156
  469.3 13.5 %all-to-all-start.1 = ((bf16[16,2,432]{2,1,0:T(2,128)(2,1)}), bf16[16,2,432]{2,1,0:T(2,128)(2,1)S(1)}, u32[]{:S(2)}, u32[]{:S(2)}) async-start(bf16[16,2,432]{2,1,0:T(2,128)(2,1)} %reshape.302), calls=%async_computation.1 | async-start | bytes 65536 | tf_op jit(solution)/shard_map/all_to_all | solution.py:107
Sparse Core Ops, SparseCore 0:
  16.3 115.2 reduce-scatter.6
  285.0 39.9 all-reduce.6
  327.8 139.3 all-reduce.4
where the time goes:
time: 492 us; the launch traced here: 491 us
  waiting for transfers between devices  293 us (60%)
  blocking collectives  140 us (28%)
  local copies, waits for them, and re-layouts  20.6 us (4%)
  between operations  14.7 us (3%)
  matrix products  9.36 us (2%)
  starting transfers between devices  7.38 us (2%)
  other arithmetic  5.83 us (1%)
    unnamed x5, waiting for transfers between devices  250 us
    all_gather x1, blocking collectives, local(): piece = lax.all_gather(arrived, 'heads', axis=2, tiled=True)  80.7 us
    psum x1, blocking collectives, local(): sum_squares = lax.psum(jnp.sum(stream * stream, 1), ('heads', 'side'))  45.8 us
    psum x1, waiting for transfers between devices, local(): lax.psum(up_part.astype(jnp.bfloat16), 'side').astype(jnp.float32)  36.9 us
    all_to_all x1, blocking collectives, local(): lax.all_to_all(holder.at[target].set(mixed_in[source_row]).reshape(groups...  13.3 us
  transfers between devices with their start and end apart: 4, of which 4 were waited for; matrix products, arithmetic and copies ran while one was open for 2% of the time, Pallas kernels for 0%

commit v1 on v0

v1 whole, which is shorter than its diff:
```python
import functools

import jax
import jax.numpy as jnp
from jax import lax
from jax.experimental import pallas as pl
from jax.experimental.pallas import tpu as pltpu
from jax.sharding import PartitionSpec as P

F32 = jnp.float32
BF16 = jnp.bfloat16
MESH = pl.DeviceIdType.MESH
SLOTS = 8
LANES = 128
IN_NAMES = ("q", "k", "v", "hg", "res", "ng", "ids", "gates", "state", "wo", "wg", "wu", "wd")


def dot(a, b):
    return jnp.dot(a, b, preferred_element_type=F32)


def kernel(dims, *refs):
    (experts, depth, rows_y, requests, steps, top, piece, hidden, width) = dims
    tokens = requests * steps
    feats = depth * piece
    groups = feats // LANES
    row_tiles = tokens // 8
    tiles = groups * row_tiles
    per = -(-tiles // depth)
    n_in = len(IN_NAMES)
    hbm = dict(zip(IN_NAMES, refs[:n_in]))
    slope_ref, state_out, resid_out, moe_out = refs[n_in : n_in + 4]
    vm = dict(zip(IN_NAMES, refs[n_in + 4 : 2 * n_in + 4]))
    (
        wdd, snew, ex_src, ex_dst, part, tsum, rs_buf, disp, dispo, recv, recvo,
        xg, ss_src, ss_dst, gu_src, gu_dst, back, backo, comb, combo, rs2_src, rs2_buf,
        in_sem, st_sem, side_send, side_recv, z_send, z_recv, dp_send, dp_recv,
    ) = refs[2 * n_in + 4 :]

    my_dp = lax.axis_index("dp")
    my_z = lax.axis_index("heads")
    my_side = lax.axis_index("side")
    partner = (my_dp, my_z, 1 - my_side)

    def z_peer(i):
        d = depth // 2 - (i + 1) // 2
        sign = 1 - 2 * ((i + 1) % 2)
        return (my_z + sign * d + depth) % depth

    def dp_peer(i):
        cols = experts // rows_y
        x = (my_dp // rows_y + i // rows_y) % cols
        y = (my_dp % rows_y + i % rows_y) % rows_y
        return x * rows_y + y

    def loads(name):
        i = IN_NAMES.index(name)
        return pltpu.make_async_copy(hbm[name], vm[name], in_sem.at[i])

    for name in ("state", "q", "k", "v", "hg", "wo", "res", "ids", "gates", "ng", "wg", "wu", "wd"):
        loads(name).start()

    barrier = pltpu.get_barrier_semaphore()

    def greet_z(i, c):
        pl.semaphore_signal(barrier, 1, device_id=(my_dp, z_peer(i), my_side), device_id_type=MESH)
        return c

    def greet_dp(i, c):
        pl.semaphore_signal(barrier, 1, device_id=(dp_peer(i), my_z, my_side), device_id_type=MESH)
        return c

    lax.fori_loop(0, depth - 1, greet_z, 0)
    lax.fori_loop(1, experts, greet_dp, 0)
    pl.semaphore_signal(barrier, 1, device_id=partner, device_id_type=MESH)

    for name in ("q", "k", "v", "hg", "state"):
        loads(name).wait()
    decay = jnp.exp(jnp.full((1, LANES), -slope_ref[0], F32))
    q = vm["q"][...].astype(F32)
    k = vm["k"][...].astype(F32)
    v = vm["v"][...].astype(F32)
    q1, q2 = q[:, 0, :], q[:, 1, :]
    k1, k2 = k[:, 0, :], k[:, 1, :]
    v1, v2 = v[:, 0, :], v[:, 1, :]
    read = jnp.einsum(
        "rsi,rij->rsj", vm["q"][...], vm["state"][...].reshape(requests, LANES, LANES),
        preferred_element_type=F32,
    )
    dotted = lambda a, b: jnp.sum(a * b, 1, keepdims=True)
    o1 = decay * read[:, 0, :] + dotted(q1, k1) * v1
    o2 = decay * decay * read[:, 1, :] + decay * (dotted(q2, k1) * v1) + dotted(q2, k2) * v2
    out = jnp.concatenate([o1, o2], 0)
    normed = out * lax.rsqrt(jnp.mean(out * out, 1, keepdims=True) + 1e-6) * vm["hg"][...]
    loads("wo").wait()
    projected = dot(normed.astype(BF16), vm["wo"][...])
    halves = [
        jnp.concatenate(
            [projected[:, (2 * a + s) * piece : (2 * a + s + 1) * piece] for a in range(depth)], 1
        )
        for s in range(2)
    ]
    first = my_side == 0
    ex_src[...] = jnp.where(first, halves[1], halves[0]).astype(BF16)
    own = jnp.where(first, halves[0], halves[1])

    pl.semaphore_wait(barrier, depth + experts - 1)

    def to_partner(src, dst, i):
        return pltpu.make_async_remote_copy(
            src_ref=src, dst_ref=dst, send_sem=side_send.at[i], recv_sem=side_recv.at[i],
            device_id=partner, device_id_type=MESH,
        )

    exchange = to_partner(ex_src, ex_dst, 0)
    exchange.start()

    loads("res").wait()
    res = vm["res"][...].astype(F32)
    res = jnp.concatenate([res[:, s, :] for s in range(steps)], 0).astype(BF16)
    place = (
        lax.broadcasted_iota(jnp.int32, (piece, feats), 1)
        == lax.broadcasted_iota(jnp.int32, (piece, feats), 0) + my_z * piece
    ).astype(BF16)
    own = own + dot(res, place)
    exchange.wait()
    chip = own + ex_dst[...].astype(F32)
    for g in range(groups):
        block = chip[:, g * LANES : (g + 1) * LANES].reshape(row_tiles, 8, LANES)
        part[g * row_tiles : (g + 1) * row_tiles] = block.astype(BF16)
    if per * depth > tiles:
        part[tiles:] = jnp.zeros((per * depth - tiles, 8, LANES), BF16)

    def z_copy(phase, src, dst, i, peer):
        return pltpu.make_async_remote_copy(
            src_ref=src, dst_ref=dst, send_sem=z_send.at[phase, i], recv_sem=z_recv.at[phase, i],
            device_id=(my_dp, peer, my_side), device_id_type=MESH,
        )

    def rs_copy(i):
        peer = z_peer(i)
        return z_copy(0, part.at[pl.ds(peer * per, per)], rs_buf.at[i], i, peer)

    def rs_start(i, c):
        rs_copy(i).start()
        return c

    lax.fori_loop(0, depth - 1, rs_start, 0)

    kd = decay * k1
    kd_hi = kd.astype(BF16).astype(F32)
    lhs = jnp.stack([kd_hi, kd - kd_hi, k2], 1).astype(BF16)
    rhs = jnp.stack([v1, v1, v2], 1).astype(BF16)
    decay2 = decay * decay
    for r in range(requests):
        outer = lax.dot_general(
            lhs[r], rhs[r], (((0,), (0,)), ((), ())), preferred_element_type=F32
        )
        snew[r, 0] = (decay2 * vm["state"][r, 0].astype(F32) + outer).astype(BF16)
    state_copy = pltpu.make_async_copy(snew, state_out, st_sem)
    state_copy.start()

    loads("ids").wait()
    loads("gates").wait()
    row_e = lax.broadcasted_iota(jnp.int32, (experts, requests), 0).astype(F32)
    row_m = lax.broadcasted_iota(jnp.int32, (experts * SLOTS, requests), 0).astype(F32)
    upper = (
        lax.broadcasted_iota(jnp.int32, (requests, requests), 0)
        < lax.broadcasted_iota(jnp.int32, (requests, requests), 1)
    ).astype(BF16)
    taken = jnp.zeros((experts, 1), F32)
    sels, selos, weights, weightos = [], [], [], []
    for s in range(steps):
        sel = jnp.zeros((experts * SLOTS, requests), F32)
        selo = jnp.zeros((experts, requests), F32)
        wsel, wselo = sel, selo
        for c in range(top):
            ids = vm["ids"][s, c : c + 1, :].astype(F32)
            gate = vm["gates"][s, c : c + 1, :]
            onehot = (row_e == ids).astype(F32)
            before = dot(onehot.astype(BF16), upper) + taken
            slot = jnp.sum(onehot * before, 0, keepdims=True)
            taken = taken + jnp.sum(onehot, 1, keepdims=True)
            hit = (row_m == jnp.where(slot < SLOTS, ids * SLOTS + slot, -1.0)).astype(F32)
            hito = (row_e == jnp.where(slot < SLOTS, -1.0, ids)).astype(F32)
            sel, selo = sel + hit, selo + hito
            wsel, wselo = wsel + hit * gate, wselo + hito * gate
        sels.append(sel)
        selos.append(selo)
        weights.append(wsel)
        weightos.append(wselo)
    sel = jnp.concatenate(sels, 1).astype(BF16)
    selo = jnp.concatenate(selos, 1).astype(BF16)
    weight = jnp.concatenate(weights, 1)
    weighto = jnp.concatenate(weightos, 1)

    loads("wd").wait()
    for a in range(depth):
        wdd[:, a * piece : (a + 1) * piece] = vm["wd"][:, a, :]

    def rs_done(i, acc):
        i = depth - 2 - i
        rs_copy(i).wait()
        return acc + rs_buf[i].astype(F32)

    mine = pl.ds(my_z * per, per)
    total = lax.fori_loop(0, depth - 1, rs_done, part[mine].astype(F32))
    tsum[mine] = total.astype(BF16)

    def ag_copy(i, wait=False):
        peer = z_peer(i)
        origin = (2 * my_z - peer + depth) % depth if wait else my_z
        there = tsum.at[pl.ds(origin * per, per)]
        return z_copy(1, there, there, i, peer)

    def ag_start(i, c):
        ag_copy(i).start()
        return c

    def ag_done(i, c):
        i = depth - 2 - i
        ag_copy(i).wait_send()
        ag_copy(i, True).wait_recv()
        return c

    lax.fori_loop(0, depth - 1, ag_start, 0)
    loads("ng").wait()
    gain = jnp.concatenate(
        [
            jnp.where(
                first,
                vm["ng"][:, 2 * a * piece : (2 * a + 1) * piece],
                vm["ng"][:, (2 * a + 1) * piece : (2 * a + 2) * piece],
            )
            for a in range(depth)
        ],
        1,
    )
    lax.fori_loop(0, depth - 1, ag_done, 0)

    cols = []
    for g in range(groups):
        block = tsum[g * row_tiles : (g + 1) * row_tiles].astype(F32)
        cols.append(block.reshape(tokens, LANES).astype(BF16))
    stream = jnp.concatenate(cols, 1)
    disp[...] = dot(sel, stream).reshape(experts, SLOTS, feats).astype(BF16)
    over = dot(selo, stream)
    for e in range(experts):
        dispo[e] = over[e : e + 1]

    def dp_copy(phase, src, dst, i, peer):
        return pltpu.make_async_remote_copy(
            src_ref=src, dst_ref=dst, send_sem=dp_send.at[phase, i], recv_sem=dp_recv.at[phase, i],
            device_id=(peer, my_z, my_side), device_id_type=MESH,
        )

    def go_copies(i):
        peer = dp_peer(i)
        return (
            dp_copy(0, disp.at[peer], recv.at[i], i, peer),
            dp_copy(1, dispo.at[peer], recvo.at[i], i, peer),
        )

    def go_start(i, c):
        for copy in go_copies(i):
            copy.start()
        return c

    def go_done(i, c):
        for copy in go_copies(i):
            copy.wait()
        return c

    lax.fori_loop(1, experts, go_start, 0)
    recv[0] = disp[my_dp]
    recvo[0] = dispo[my_dp]
    resid_out[...] = lax.dot_general(
        stream, place, (((1,), (1,)), ((), ())), preferred_element_type=F32
    ).astype(BF16)
    loads("wg").wait()
    loads("wu").wait()
    lax.fori_loop(1, experts, go_done, 0)

    main = experts * SLOTS
    slots = main + experts
    for j in range(experts // 2 + experts // 16 + (1 if experts % 16 else 0)):
        lo = 16 * j
        if lo < main:
            x = recv[2 * j : 2 * j + 2].astype(F32).reshape(16, feats)
            n = 16
        else:
            x = jnp.concatenate([recvo[e] for e in range(experts)], 0)
            n = experts
        squares = jnp.sum(x * x, 1, keepdims=True)
        ss_src[lo : lo + n, :] = jnp.broadcast_to(squares, (n, LANES))
        xg[lo : lo + n, :] = (x * gain).astype(BF16)
    gate_own = dot(xg[...], vm["wg"][...].reshape(feats, hidden))
    gu_src[0] = gate_own.astype(BF16)
    up_own = dot(xg[...], vm["wu"][...].reshape(feats, hidden))
    gu_src[1] = up_own.astype(BF16)
    gu_copy = to_partner(gu_src, gu_dst, 1)
    ss_copy = to_partner(ss_src, ss_dst, 2)
    gu_copy.start()
    ss_copy.start()
    gu_copy.wait()
    ss_copy.wait()
    scale = lax.rsqrt((ss_src[...] + ss_dst[...]) / width + 1e-6)[:, :1]
    gate_val = (gate_own + gu_dst[0].astype(F32)) * scale
    up_val = (up_own + gu_dst[1].astype(F32)) * scale
    act = (gate_val / (1.0 + jnp.exp(-gate_val)) * up_val).astype(BF16)

    down = dot(act, wdd[...])
    back[...] = down[:main].reshape(experts, SLOTS, feats).astype(BF16)
    for e in range(experts):
        backo[e] = down[main + e : main + e + 1]

    def home(i):
        cols = experts // rows_y
        x = (my_dp // rows_y - i // rows_y + cols) % cols
        y = (my_dp % rows_y - i % rows_y + rows_y) % rows_y
        return x * rows_y + y

    def back_copies(i, wait=False):
        peer = home(i)
        slot = dp_peer(i) if wait else my_dp
        return (
            dp_copy(2, back.at[i], comb.at[slot], i, peer),
            dp_copy(3, backo.at[i], combo.at[slot], i, peer),
        )

    def back_start(i, c):
        for copy in back_copies(i):
            copy.start()
        return c

    def back_done(i, c):
        for copy in back_copies(i):
            copy.wait_send()
        for copy in back_copies(i, True):
            copy.wait_recv()
        return c

    lax.fori_loop(1, experts, back_start, 0)
    comb[my_dp] = back[0]
    combo[my_dp] = backo[0]
    w_hi = weight.astype(BF16)
    w_lo = (weight - w_hi.astype(F32)).astype(BF16)
    lax.fori_loop(1, experts, back_done, 0)

    tdot = lambda a, b: lax.dot_general(a, b, (((0,), (0,)), ((), ())), preferred_element_type=F32)
    got = comb[...].astype(F32).reshape(main, feats).astype(BF16)
    goto = jnp.concatenate([combo[e] for e in range(experts)], 0).astype(BF16)
    mixed = tdot(w_hi, got) + tdot(w_lo, got) + tdot(weighto.astype(BF16), goto)

    for a in range(depth):
        rs2_src[a] = mixed[:, a * piece : (a + 1) * piece].astype(BF16)

    def rs2_copy(i):
        peer = z_peer(i)
        return z_copy(2, rs2_src.at[peer], rs2_buf.at[i], i, peer)

    def rs2_start(i, c):
        rs2_copy(i).start()
        return c

    def rs2_done(i, acc):
        i = depth - 2 - i
        rs2_copy(i).wait()
        return acc + rs2_buf[i].astype(F32)

    lax.fori_loop(0, depth - 1, rs2_start, 0)
    final = lax.fori_loop(0, depth - 1, rs2_done, rs2_src[my_z].astype(F32))
    moe_out[...] = final.astype(BF16)
    state_copy.wait()


def layer(mesh_shape, q, k, v, state, slopes, hg, wo, res, ng, ids, gates, wg, wu, wd):
    experts, depth = mesh_shape["dp"], mesh_shape["heads"]
    requests, steps, head = q.shape
    piece = res.shape[2]
    hidden = wg.shape[3]
    top = ids.shape[2]
    width = ng.shape[0]
    tokens = requests * steps
    feats = depth * piece
    per = -(-(feats // LANES) * (tokens // 8) // depth)
    main = experts * SLOTS
    slots = main + experts
    rows_y = 4 if experts == 16 else experts
    dims = (experts, depth, rows_y, requests, steps, top, piece, hidden, width)
    operands = {
        "q": q, "k": k, "v": v, "hg": hg.reshape(1, head), "res": res, "ng": ng.reshape(1, width),
        "ids": ids.transpose(1, 2, 0), "gates": gates.transpose(1, 2, 0), "state": state, "wo": wo,
        "wg": wg[0], "wu": wu[0], "wd": wd[0],
    }
    arrays = [operands[name] for name in IN_NAMES]
    dma = pltpu.SemaphoreType.DMA
    scratch = [pltpu.VMEM(a.shape, a.dtype) for a in arrays] + [
        pltpu.VMEM((hidden, feats), BF16),
        pltpu.VMEM(state.shape, BF16),
        pltpu.VMEM((tokens, feats), BF16),
        pltpu.VMEM((tokens, feats), BF16),
        pltpu.VMEM((per * depth, 8, LANES), BF16),
        pltpu.VMEM((per * depth, 8, LANES), BF16),
        pltpu.VMEM((depth - 1, per, 8, LANES), BF16),
        pltpu.VMEM((experts, SLOTS, feats), BF16),
        pltpu.VMEM((experts, 1, feats), F32),
        pltpu.VMEM((experts, SLOTS, feats), BF16),
        pltpu.VMEM((experts, 1, feats), F32),
        pltpu.VMEM((slots, feats), BF16),
        pltpu.VMEM((slots, LANES), F32),
        pltpu.VMEM((slots, LANES), F32),
        pltpu.VMEM((2, slots, hidden), BF16),
        pltpu.VMEM((2, slots, hidden), BF16),
        pltpu.VMEM((experts, SLOTS, feats), BF16),
        pltpu.VMEM((experts, 1, feats), F32),
        pltpu.VMEM((experts, SLOTS, feats), BF16),
        pltpu.VMEM((experts, 1, feats), F32),
        pltpu.VMEM((depth, tokens, piece), BF16),
        pltpu.VMEM((depth - 1, tokens, piece), BF16),
        dma((len(IN_NAMES),)),
        dma,
        dma((3,)),
        dma((3,)),
        dma((3, depth)),
        dma((3, depth)),
        dma((4, experts)),
        dma((4, experts)),
    ]
    any_spec = pl.BlockSpec(memory_space=pl.ANY)
    state_new, resid, moe = pl.pallas_call(
        functools.partial(kernel, dims),
        out_shape=(
            jax.ShapeDtypeStruct(state.shape, BF16),
            jax.ShapeDtypeStruct((tokens, piece), BF16),
            jax.ShapeDtypeStruct((tokens, piece), BF16),
        ),
        in_specs=[any_spec] * len(arrays) + [pl.BlockSpec(memory_space=pltpu.SMEM)],
        out_specs=(
            any_spec,
            pl.BlockSpec(memory_space=pltpu.VMEM),
            pl.BlockSpec(memory_space=pltpu.VMEM),
        ),
        scratch_shapes=scratch,
        compiler_params=pltpu.CompilerParams(
            collective_id=0, has_side_effects=True, vmem_limit_bytes=56 * 1024 * 1024
        ),
        name="layer",
    )(*arrays, slopes)
    back = lambda x: x.reshape(steps, requests, piece).transpose(1, 0, 2)
    return state_new, back(resid), back(moe)


def solution(mesh):
    return jax.shard_map(
        functools.partial(layer, dict(mesh.shape)),
        mesh=mesh,
        in_specs=(
            P("dp", None, ("heads", "side")),
            P("dp", None, ("heads", "side")),
            P("dp", None, ("heads", "side")),
            P("dp", ("heads", "side"), None, None),
            P(("heads", "side")),
            P(("heads", "side")),
            P(("heads", "side"), None),
            P("dp", None, ("heads", "side")),
            P(),
            P("dp", None, None),
            P("dp", None, None),
            P("dp", None, "side", "heads"),
            P("dp", None, "side", "heads"),
            P("dp", "heads", None, "side"),
        ),
        out_specs=(
            P("dp", ("heads", "side"), None, None),
            P("dp", None, ("heads", "side")),
            P("dp", None, ("heads", "side")),
        ),
        check_vma=False,
    )
```

time: 492 us -> 75.8 us (0.15)
  the two profiles are of different devices: /device:TPU:8 before, /device:TPU:6 now
where the time goes in v1:
time: 75.8 us; the launch traced here: 75.5 us
  Pallas kernels  70.8 us (93%)
  local copies, waits for them, and re-layouts  3.44 us (5%)
  between operations  1.29 us (2%)
    pallas_call x1, Pallas kernels, layer(): pl.pallas_call(functools.partial(kernel, dims), out_shape=(jax.ShapeDtype...  70.8 us
    unnamed x1, local copies, waits for them, and re-layouts  2.09 us

profile of v1, /device:TPU:6, one launch (start us, length us, event | category | flops | bytes accessed | tf_op | source)
XLA Modules:
  0.0 75.5 jit_solution(5554272610800597103)
XLA Ops:
  1.3 70.8 %layer.1 = (bf16[24,1,128,128]{3,2,1,0:T(8,128)(2,1)}, bf16[48,96]{1,0:T(8,128)(2,1)}, bf16[48,96]{1,0:T(8,128)(2,1)}) custom-call(bf16[24,2,128]{2,1,0:T(2,128)(2,1)} %refs_0_.1, bf16[24,2,128]{2,1,0:T(2,128)(2,1)} %refs_1_.1, bf16[24,2,128]{2,1,0:T(2,128)(2,1)} %refs_2_.1, f32[1,128]{1,0:T(1,128)} %bitcast.21, bf16[24,2,96]{2,1,0:T(2,128)(2,1)} %refs_4_.1, ...), custom_call_target="tpu_custom_call" | custom-call | tf_op jit(solution)/shard_map/layer/pallas_call | solution.py:431
  72.0 1.3 %copy_bitcast_fusion = (bf16[24,2,96]{2,1,0:T(2,128)(2,1)}, bf16[24,2,96]{2,1,0:T(2,128)(2,1)}) fusion(bf16[2,24,96]{2,1,0:T(8,128)(2,1)} %bitcast.17, bf16[2,24,96]{2,1,0:T(8,128)(2,1)} %bitcast.16), kind=kLoop, calls=%fused_computation | loop fusion | bytes 36864 | tf_op jit(solution)/shard_map/transpose | solution.py:450
  73.4 2.1 %copy.23 = bf16[24,1,128,128]{3,2,1,0:T(8,128)(2,1)} copy(bf16[24,1,128,128]{3,2,1,0:T(8,128)(2,1)} %get-tuple-element.14) | data formatting | bytes 1572864

commit v2 on v1

v2 whole, which is shorter than its diff:
```python
import functools

import jax
import jax.numpy as jnp
from jax import lax
from jax.experimental import pallas as pl
from jax.experimental.pallas import tpu as pltpu
from jax.sharding import PartitionSpec as P

F32 = jnp.float32
BF16 = jnp.bfloat16
MESH = pl.DeviceIdType.MESH
SLOTS = 8
LANES = 128
IN_NAMES = ("q", "k", "v", "hg", "res", "ng", "ids", "gates", "state", "wo", "wg", "wu", "wd")


def dot(a, b):
    return jnp.dot(a, b, preferred_element_type=F32)


def kernel(dims, *refs):
    (experts, depth, chunks, rows_y, requests, steps, top, piece, hidden, width) = dims
    tokens = requests * steps
    span = depth // chunks
    wide = span * piece
    lane_groups = wide // LANES
    row_tiles = tokens // 8
    tiles = lane_groups * row_tiles
    per = -(-tiles // span)
    feats = depth * piece
    main = experts * SLOTS
    slots = main + experts
    n_in = len(IN_NAMES)
    hbm = dict(zip(IN_NAMES, refs[:n_in]))
    slope_ref, state_out, resid_out, moe_out = refs[n_in : n_in + 4]
    vm = dict(zip(IN_NAMES, refs[n_in + 4 : 2 * n_in + 4]))
    (
        wdd, ex_src, ex_dst, part, tsum, rs_buf, disp, recv, gain_v,
        ss_src, ss_dst, gu_src, gu_dst, back, comb, rs2_src, rs2_buf,
        in_sem, side_send, side_recv, z_send, z_recv, dp_send, dp_recv,
    ) = refs[2 * n_in + 4 :]

    my_dp = lax.axis_index("dp")
    my_z = lax.axis_index("heads")
    my_side = lax.axis_index("side")
    partner = (my_dp, my_z, 1 - my_side)
    my_chunk = my_z // span
    ahead = [(chunks // 2 + (p + 1) // 2 * (1 - 2 * (p % 2)) + chunks) % chunks for p in range(chunks)]
    order = [(my_chunk + shift) % chunks for shift in ahead]

    def z_peer(i):
        d = depth // 2 - (i + 1) // 2
        sign = 1 - 2 * ((i + 1) % 2)
        return (my_z + sign * d + depth) % depth

    columns = experts // rows_y

    def dp_peer(i):
        x = (my_dp // rows_y + i // rows_y) % columns
        y = (my_dp % rows_y + i % rows_y) % rows_y
        return x * rows_y + y

    def home(i):
        x = (my_dp // rows_y - i // rows_y + columns) % columns
        y = (my_dp % rows_y - i % rows_y + rows_y) % rows_y
        return x * rows_y + y

    def loads(name):
        i = IN_NAMES.index(name)
        return pltpu.make_async_copy(hbm[name], vm[name], in_sem.at[i])

    def to_partner(src, dst, i):
        return pltpu.make_async_remote_copy(
            src_ref=src, dst_ref=dst, send_sem=side_send.at[i], recv_sem=side_recv.at[i],
            device_id=partner, device_id_type=MESH,
        )

    def z_copy(phase, src, dst, peer):
        return pltpu.make_async_remote_copy(
            src_ref=src, dst_ref=dst, send_sem=z_send.at[phase], recv_sem=z_recv.at[phase],
            device_id=(my_dp, peer, my_side), device_id_type=MESH,
        )

    def dp_copy(phase, src, dst, peer):
        return pltpu.make_async_remote_copy(
            src_ref=src, dst_ref=dst, send_sem=dp_send.at[phase], recv_sem=dp_recv.at[phase],
            device_id=(peer, my_z, my_side), device_id_type=MESH,
        )

    for name in ("state", "q", "k", "v", "hg", "wo", "wd", "res", "ids", "gates", "ng", "wg", "wu"):
        loads(name).start()

    barrier = pltpu.get_barrier_semaphore()

    def greet_z(i, c):
        pl.semaphore_signal(barrier, 1, device_id=(my_dp, z_peer(i), my_side), device_id_type=MESH)
        return c

    def greet_dp(i, c):
        pl.semaphore_signal(barrier, 1, device_id=(dp_peer(i), my_z, my_side), device_id_type=MESH)
        return c

    lax.fori_loop(0, depth - 1, greet_z, 0)
    lax.fori_loop(1, experts, greet_dp, 0)
    pl.semaphore_signal(barrier, 1, device_id=partner, device_id_type=MESH)

    for name in ("q", "k", "v", "hg", "state"):
        loads(name).wait()
    decay = jnp.exp(jnp.full((1, LANES), -slope_ref[0], F32))
    q = vm["q"][...].astype(F32)
    k = vm["k"][...].astype(F32)
    v = vm["v"][...].astype(F32)
    q1, q2 = q[:, 0, :], q[:, 1, :]
    k1, k2 = k[:, 0, :], k[:, 1, :]
    v1, v2 = v[:, 0, :], v[:, 1, :]
    read = jnp.einsum(
        "rsi,rij->rsj", vm["q"][...], vm["state"][...].reshape(requests, LANES, LANES),
        preferred_element_type=F32,
    )
    dotted = lambda a, b: jnp.sum(a * b, 1, keepdims=True)
    o1 = decay * read[:, 0, :] + dotted(q1, k1) * v1
    o2 = decay * decay * read[:, 1, :] + decay * (dotted(q2, k1) * v1) + dotted(q2, k2) * v2
    out = jnp.concatenate([o1, o2], 0)
    normed = out * lax.rsqrt(jnp.mean(out * out, 1, keepdims=True) + 1e-6) * vm["hg"][...]
    loads("wo").wait()
    projected = dot(normed.astype(BF16), vm["wo"][...])
    halves = [
        jnp.concatenate(
            [projected[:, (2 * a + s) * piece : (2 * a + s + 1) * piece] for a in range(depth)], 1
        )
        for s in range(2)
    ]
    first = my_side == 0
    ex_src[...] = jnp.where(first, halves[1], halves[0]).astype(BF16)
    own = jnp.where(first, halves[0], halves[1])

    loads("res").wait()
    res = vm["res"][...].astype(F32)
    res = jnp.concatenate([res[:, s, :] for s in range(steps)], 0).astype(BF16)

    def placed(size, at):
        column = lax.broadcasted_iota(jnp.int32, (piece, size), 1)
        row = lax.broadcasted_iota(jnp.int32, (piece, size), 0)
        return (column == row + at * piece).astype(BF16)

    own = own + dot(res, placed(feats, my_z))

    loads("wd").wait()
    for a in range(depth):
        at = a % span * piece
        wdd[a // span, :, at : at + piece] = vm["wd"][:, a, :]

    pl.semaphore_wait(barrier, depth + experts - 1)
    exchange = to_partner(ex_src, ex_dst, 0)
    exchange.start()

    loads("ids").wait()
    loads("gates").wait()
    row_e = lax.broadcasted_iota(jnp.int32, (experts, requests), 0).astype(F32)
    row_m = lax.broadcasted_iota(jnp.int32, (main, requests), 0).astype(F32)
    upper = (
        lax.broadcasted_iota(jnp.int32, (requests, requests), 0)
        < lax.broadcasted_iota(jnp.int32, (requests, requests), 1)
    ).astype(BF16)
    taken = jnp.zeros((experts, 1), F32)
    kinds = 1 + lane_groups
    picks = [[] for _ in range(kinds)]
    shares = [[] for _ in range(kinds)]
    for s in range(steps):
        pick = [jnp.zeros((main, requests), F32) for _ in range(kinds)]
        share = list(pick)
        for c in range(top):
            ids = vm["ids"][s, c : c + 1, :].astype(F32)
            gate = vm["gates"][s, c : c + 1, :]
            onehot = (row_e == ids).astype(F32)
            before = dot(onehot.astype(BF16), upper) + taken
            slot = jnp.sum(onehot * before, 0, keepdims=True)
            taken = taken + jnp.sum(onehot, 1, keepdims=True)
            low = slot < SLOTS
            goals = [jnp.where(low, ids * SLOTS + slot, -1.0)]
            goals += [jnp.where(low, -1.0, ids * SLOTS + j) for j in range(lane_groups)]
            for n, goal in enumerate(goals):
                hit = (row_m == goal).astype(F32)
                pick[n] = pick[n] + hit
                share[n] = share[n] + hit * gate
        for n in range(kinds):
            picks[n].append(pick[n])
            shares[n].append(share[n])
    picks = [jnp.concatenate(p, 1).astype(BF16) for p in picks]

    def split(x):
        high = x.astype(BF16)
        return jnp.concatenate([high, (x - high.astype(F32)).astype(BF16)], 1)

    shares = [split(jnp.concatenate(s, 1).T) for s in shares]
    loads("ng").wait()
    for a in range(depth):
        at = a % span * piece
        gain_v[a // span, :, at : at + piece] = jnp.where(
            first,
            vm["ng"][:, 2 * a * piece : (2 * a + 1) * piece],
            vm["ng"][:, (2 * a + 1) * piece : (2 * a + 2) * piece],
        )
    exchange.wait()
    chip = own + ex_dst[...].astype(F32)
    for c in range(chunks):
        base = c * span * per
        for j in range(lane_groups):
            at = c * wide + j * LANES
            block = chip[:, at : at + LANES].reshape(row_tiles, 8, LANES)
            part[base + j * row_tiles : base + (j + 1) * row_tiles] = block.astype(BF16)
        if span * per > tiles:
            part[base + tiles : base + span * per] = jnp.zeros((span * per - tiles, 8, LANES), BF16)

    def rs_start(i, c):
        peer = z_peer(i)
        z_copy(0, part.at[pl.ds(peer * per, per)], rs_buf.at[i], peer).start()
        return c

    lax.fori_loop(0, depth - 1, rs_start, 0)

    kd = decay * k1
    kd_hi = kd.astype(BF16).astype(F32)
    lhs = jnp.stack([kd_hi, kd - kd_hi, k2], 1).astype(BF16)
    rhs = jnp.stack([v1, v1, v2], 1).astype(BF16)
    decay2 = decay * decay
    for r in range(requests):
        outer = lax.dot_general(
            lhs[r], rhs[r], (((0,), (0,)), ((), ())), preferred_element_type=F32
        )
        state_out[r, 0] = (decay2 * vm["state"][r, 0].astype(F32) + outer).astype(BF16)

    z_copy(0, rs_buf, rs_buf, z_peer(0)).wait()
    mine = pl.ds(my_z * per, per)
    total = part[mine].astype(F32)
    for i in range(depth - 1):
        total = total + rs_buf[i].astype(F32)
    tsum[mine] = total.astype(BF16)

    def ag_start(i, c):
        peer = z_peer(i)
        pltpu.make_async_remote_copy(
            src_ref=tsum.at[mine], dst_ref=tsum.at[mine], send_sem=z_send.at[1],
            recv_sem=z_recv.at[3 + my_chunk], device_id=(my_dp, peer, my_side), device_id_type=MESH,
        ).start()
        return c

    lax.fori_loop(0, depth - 1, ag_start, 0)

    for p, chunk in enumerate(order):
        count = span * per if ahead[p] else (span - 1) * per
        held = tsum.at[pl.ds(0, count)]
        if count:
            pltpu.make_async_remote_copy(
                src_ref=held, dst_ref=held, send_sem=z_send.at[1], recv_sem=z_recv.at[3 + chunk],
                device_id=partner, device_id_type=MESH,
            ).wait_recv()
        cols = []
        for j in range(lane_groups):
            block = tsum[pl.ds(chunk * span * per + j * row_tiles, row_tiles)].astype(F32)
            cols.append(block.reshape(tokens, LANES).astype(BF16))
        last = jnp.zeros((main, LANES), F32)
        for j, col in enumerate(cols):
            disp[p, :, j] = dot(picks[0], col).reshape(experts, SLOTS, LANES).astype(BF16)
            last = last + dot(picks[1 + j], col)
        disp[p, :, lane_groups] = last.reshape(experts, SLOTS, LANES).astype(BF16)

        def go_start(i, c, p=p):
            peer = dp_peer(i)
            dp_copy(p, disp.at[p, peer], recv.at[p, i], peer).start()
            return c

        lax.fori_loop(1, experts, go_start, 0)
        recv[p, 0] = disp[p, my_dp]
        if not ahead[p]:
            resid_out[...] = lax.dot_general(
                jnp.concatenate(cols, 1), placed(wide, my_z % span),
                (((1,), (1,)), ((), ())), preferred_element_type=F32,
            ).astype(BF16)

    z_copy(1, rs_buf, rs_buf, z_peer(0)).wait_send()
    loads("wg").wait()
    loads("wu").wait()
    unpick = [
        (
            lax.broadcasted_iota(jnp.int32, (experts, main), 1)
            == lax.broadcasted_iota(jnp.int32, (experts, main), 0) * SLOTS + j
        ).astype(BF16)
        for j in range(lane_groups)
    ]
    others = pl.ds(1, experts - 1)
    gate_own = jnp.zeros((slots, hidden), F32)
    up_own = jnp.zeros((slots, hidden), F32)
    squares = jnp.zeros((slots, LANES), F32)
    for p, chunk in enumerate(order):
        dp_copy(p, disp.at[p, others], recv.at[p, others], dp_peer(1)).wait()
        last = recv[p, :, lane_groups].astype(F32).reshape(main, LANES).astype(BF16)
        xs = []
        for j in range(lane_groups):
            x = jnp.concatenate(
                [recv[p, :, j].astype(F32).reshape(main, LANES), dot(unpick[j], last)], 0
            )
            squares = squares + x * x
            xs.append((x * gain_v[chunk][:, j * LANES : (j + 1) * LANES]).astype(BF16))
        x = jnp.concatenate(xs, 1)
        rows = pl.ds(chunk * span, span)
        gate_own = gate_own + dot(x, vm["wg"][rows].reshape(wide, hidden))
        up_own = up_own + dot(x, vm["wu"][rows].reshape(wide, hidden))
    gu_src[0] = gate_own.astype(BF16)
    gu_src[1] = up_own.astype(BF16)
    ss_src[...] = jnp.broadcast_to(jnp.sum(squares, 1, keepdims=True), (slots, LANES))
    gu_copy = to_partner(gu_src, gu_dst, 1)
    ss_copy = to_partner(ss_src, ss_dst, 2)
    gu_copy.start()
    ss_copy.start()
    ss_copy.wait()
    scale = lax.rsqrt((ss_src[...] + ss_dst[...]) / width + 1e-6)[:, :1]
    gu_copy.wait()
    gate_val = (gate_own + gu_dst[0].astype(F32)) * scale
    up_val = (up_own + gu_dst[1].astype(F32)) * scale
    act = (gate_val / (1.0 + jnp.exp(-gate_val)) * up_val).astype(BF16)

    for p, chunk in enumerate(order):
        down = dot(act, wdd[chunk])
        last = jnp.zeros((main, LANES), F32)
        for j in range(lane_groups):
            col = down[:, j * LANES : (j + 1) * LANES]
            back[p, :, j] = col[:main].reshape(experts, SLOTS, LANES).astype(BF16)
            last = last + lax.dot_general(
                unpick[j], col[main:].astype(BF16), (((0,), (0,)), ((), ())),
                preferred_element_type=F32,
            )
        back[p, :, lane_groups] = last.reshape(experts, SLOTS, LANES).astype(BF16)

        def back_start(i, c, p=p):
            dp_copy(chunks + p, back.at[p, i], comb.at[p, my_dp], home(i)).start()
            return c

        lax.fori_loop(1, experts, back_start, 0)
        comb[p, my_dp] = back[p, 0]

    for p, chunk in enumerate(order):
        dp_copy(chunks + p, back.at[p, others], comb.at[p, others], dp_peer(1)).wait()
        last = comb[p, :, lane_groups].astype(F32).reshape(main, LANES).astype(BF16)
        twice = jnp.concatenate([last, last], 0)
        cols = []
        for j in range(lane_groups):
            got = comb[p, :, j].astype(F32).reshape(main, LANES).astype(BF16)
            got = jnp.concatenate([got, got], 0)
            cols.append(dot(shares[0], got) + dot(shares[1 + j], twice))
        mixed = jnp.concatenate(cols, 1)
        for b in range(span):
            lanes = [
                mixed[t * 8 : t * 8 + 8, b * piece : (b + 1) * piece] for t in range(row_tiles)
            ]
            pad = rs2_buf.shape[2] - row_tiles * piece
            if pad:
                lanes.append(jnp.zeros((8, pad), F32))
            rs2_src[p, b] = jnp.concatenate(lanes, 1).astype(BF16)
        for b in range(span):
            peer = chunk * span + b

            def send(p=p, b=b, peer=peer):
                z_copy(2, rs2_src.at[p, b], rs2_buf.at[my_z], peer).start()

            if ahead[p]:
                send()
            else:
                pl.when(peer != my_z)(send)
    rs2_buf[my_z] = rs2_src[chunks - 1, my_z % span]
    arrived = rs2_buf.at[pl.ds(0, depth - 1)]
    z_copy(2, arrived, arrived, z_peer(0)).wait()
    final = rs2_buf[0].astype(F32)
    for i in range(1, depth):
        final = final + rs2_buf[i].astype(F32)
    for t in range(row_tiles):
        moe_out[t * 8 : t * 8 + 8, :] = final[:, t * piece : (t + 1) * piece].astype(BF16)


def layer(mesh_shape, q, k, v, state, slopes, hg, wo, res, ng, ids, gates, wg, wu, wd):
    experts, depth = mesh_shape["dp"], mesh_shape["heads"]
    requests, steps, head = q.shape
    piece = res.shape[2]
    hidden = wg.shape[3]
    top = ids.shape[2]
    width = ng.shape[0]
    tokens = requests * steps
    feats = depth * piece
    chunks = max(1, depth // 4)
    span = depth // chunks
    wide = span * piece
    per = -(-(wide // LANES) * (tokens // 8) // span)
    slots = experts * SLOTS + experts
    packed = -(-(tokens // 8) * piece // LANES) * LANES
    tiled = (chunks, experts, wide // LANES + 1, SLOTS, LANES)
    rows_y = 4 if experts == 16 else experts
    dims = (experts, depth, chunks, rows_y, requests, steps, top, piece, hidden, width)
    operands = {
        "q": q, "k": k, "v": v, "hg": hg.reshape(1, head), "res": res, "ng": ng.reshape(1, width),
        "ids": ids.transpose(1, 2, 0), "gates": gates.transpose(1, 2, 0), "state": state, "wo": wo,
        "wg": wg[0], "wu": wu[0], "wd": wd[0],
    }
    arrays = [operands[name] for name in IN_NAMES]
    dma = pltpu.SemaphoreType.DMA
    scratch = [pltpu.VMEM(a.shape, a.dtype) for a in arrays] + [
        pltpu.VMEM((chunks, hidden, wide), BF16),
        pltpu.VMEM((tokens, feats), BF16),
        pltpu.VMEM((tokens, feats), BF16),
        pltpu.VMEM((per * depth, 8, LANES), BF16),
        pltpu.VMEM((per * depth, 8, LANES), BF16),
        pltpu.VMEM((depth - 1, per, 8, LANES), BF16),
        pltpu.VMEM(tiled, BF16),
        pltpu.VMEM(tiled, BF16),
        pltpu.VMEM((chunks, 1, wide), F32),
        pltpu.VMEM((slots, LANES), F32),
        pltpu.VMEM((slots, LANES), F32),
        pltpu.VMEM((2, slots, hidden), BF16),
        pltpu.VMEM((2, slots, hidden), BF16),
        pltpu.VMEM(tiled, BF16),
        pltpu.VMEM(tiled, BF16),
        pltpu.VMEM((chunks, span, 8, packed), BF16),
        pltpu.VMEM((depth, 8, packed), BF16),
        dma((len(IN_NAMES),)),
        dma((3,)),
        dma((3,)),
        dma((3,)),
        dma((3 + chunks,)),
        dma((2 * chunks,)),
        dma((2 * chunks,)),
    ]
    any_spec = pl.BlockSpec(memory_space=pl.ANY)
    state_new, resid, moe = pl.pallas_call(
        functools.partial(kernel, dims),
        out_shape=(
            pltpu.VMEM(state.shape, BF16),
            pltpu.VMEM((tokens, piece), BF16),
            pltpu.VMEM((tokens, piece), BF16),
        ),
        in_specs=[any_spec] * len(arrays) + [pl.BlockSpec(memory_space=pltpu.SMEM)],
        out_specs=(
            pl.BlockSpec(memory_space=pltpu.VMEM),
            pl.BlockSpec(memory_space=pltpu.VMEM),
            pl.BlockSpec(memory_space=pltpu.VMEM),
        ),
        scratch_shapes=scratch,
        compiler_params=pltpu.CompilerParams(
            collective_id=0, has_side_effects=True, vmem_limit_bytes=56 * 1024 * 1024
        ),
        name="layer",
    )(*arrays, slopes)
    back = lambda x: x.reshape(steps, requests, piece).transpose(1, 0, 2)
    return state_new, back(resid), back(moe)


def solution(mesh):
    return jax.shard_map(
        functools.partial(layer, dict(mesh.shape)),
        mesh=mesh,
        in_specs=(
            P("dp", None, ("heads", "side")),
            P("dp", None, ("heads", "side")),
            P("dp", None, ("heads", "side")),
            P("dp", ("heads", "side"), None, None),
            P(("heads", "side")),
            P(("heads", "side")),
            P(("heads", "side"), None),
            P("dp", None, ("heads", "side")),
            P(),
            P("dp", None, None),
            P("dp", None, None),
            P("dp", None, "side", "heads"),
            P("dp", None, "side", "heads"),
            P("dp", "heads", None, "side"),
        ),
        out_specs=(
            P("dp", ("heads", "side"), None, None),
            P("dp", None, ("heads", "side")),
            P("dp", None, ("heads", "side")),
        ),
        check_vma=False,
    )
```

time: 75.8 us -> 65.8 us (0.87)
  the two profiles are of different devices: /device:TPU:6 before, /device:TPU:1 now
where the time goes in v2:
time: 65.8 us; the launch traced here: 64.6 us
  Pallas kernels  61.8 us (94%)
  local copies, waits for them, and re-layouts  1.5 us (2%)
  between operations  1.29 us (2%)
    pallas_call x1, Pallas kernels, layer(): pl.pallas_call(functools.partial(kernel, dims), out_shape=(pltpu.VMEM(sta...  61.8 us

profile of v2, /device:TPU:1, one launch (start us, length us, event | category | flops | bytes accessed | tf_op | source)
XLA Modules:
  0.0 64.6 jit_solution(11453186806711916056)
XLA Ops:
  1.3 61.8 %layer.1 = (bf16[24,1,128,128]{3,2,1,0:T(8,128)(2,1)S(1)}, bf16[48,96]{1,0:T(8,128)(2,1)S(1)}, bf16[48,96]{1,0:T(8,128)(2,1)S(1)}) custom-call(bf16[24,2,128]{2,1,0:T(2,128)(2,1)} %refs_0_.1, bf16[24,2,128]{2,1,0:T(2,128)(2,1)} %refs_1_.1, bf16[24,2,128]{2,1,0:T(2,128)(2,1)} %refs_2_.1, f32[1,128]{1,0:T(1,128)} %bitcast.21, bf16[24,2,96]{2,1,0:T(2,128)(2,1)} %refs_4_.1, ...), custom_call_target="tpu_custom_call" | custom-call | tf_op jit(solution)/shard_map/layer/pallas_call | solution.py:433
  63.1 0.9 %copy.22 = bf16[24,1,128,128]{3,2,1,0:T(8,128)(2,1)} copy(bf16[24,1,128,128]{3,2,1,0:T(8,128)(2,1)S(1)} %get-tuple-element.11) | data formatting | bytes 1572864
  64.0 0.6 copy_bitcast_fusion

commit v3 on v2

--- a/solution.py
+++ b/solution.py
@@ -36,8 +36,8 @@
     slope_ref, state_out, resid_out, moe_out = refs[n_in : n_in + 4]
     vm = dict(zip(IN_NAMES, refs[n_in + 4 : 2 * n_in + 4]))
     (
-        wdd, ex_src, ex_dst, part, tsum, rs_buf, disp, recv, gain_v,
-        ss_src, ss_dst, gu_src, gu_dst, back, comb, rs2_src, rs2_buf,
+        wdd, ex_src, ex_dst, part, tsum, inbox, relay, disp, recv, gain_v,
+        ss_src, ss_dst, gu_src, gu_dst, back, comb, part2, inbox2, relay2,
         in_sem, side_send, side_recv, z_send, z_recv, dp_send, dp_recv,
     ) = refs[2 * n_in + 4 :]
 
@@ -48,11 +48,12 @@
     my_chunk = my_z // span
     ahead = [(chunks // 2 + (p + 1) // 2 * (1 - 2 * (p % 2)) + chunks) % chunks for p in range(chunks)]
     order = [(my_chunk + shift) % chunks for shift in ahead]
-
-    def z_peer(i):
-        d = depth // 2 - (i + 1) // 2
-        sign = 1 - 2 * ((i + 1) % 2)
-        return (my_z + sign * d + depth) % depth
+    nearest = sorted(range(chunks), key=lambda shift: min(shift, chunks - shift))
+    near_order = [(my_chunk + shift) % chunks for shift in nearest]
+    hop = depth // 4
+
+    def z_at(offset):
+        return (my_z + offset + depth) % depth
 
     columns = experts // rows_y
 
@@ -76,12 +77,6 @@
             device_id=partner, device_id_type=MESH,
         )
 
-    def z_copy(phase, src, dst, peer):
-        return pltpu.make_async_remote_copy(
-            src_ref=src, dst_ref=dst, send_sem=z_send.at[phase], recv_sem=z_recv.at[phase],
-            device_id=(my_dp, peer, my_side), device_id_type=MESH,
-        )
-
     def dp_copy(phase, src, dst, peer):
         return pltpu.make_async_remote_copy(
             src_ref=src, dst_ref=dst, send_sem=dp_send.at[phase], recv_sem=dp_recv.at[phase],
@@ -93,15 +88,15 @@
 
     barrier = pltpu.get_barrier_semaphore()
 
-    def greet_z(i, c):
-        pl.semaphore_signal(barrier, 1, device_id=(my_dp, z_peer(i), my_side), device_id_type=MESH)
-        return c
-
     def greet_dp(i, c):
         pl.semaphore_signal(barrier, 1, device_id=(dp_peer(i), my_z, my_side), device_id_type=MESH)
         return c
 
-    lax.fori_loop(0, depth - 1, greet_z, 0)
+    for offset in range(hop, 0, -1):
+        for sign in (1, -1):
+            pl.semaphore_signal(
+                barrier, 1, device_id=(my_dp, z_at(sign * offset), my_side), device_id_type=MESH
+            )
     lax.fori_loop(1, experts, greet_dp, 0)
     pl.semaphore_signal(barrier, 1, device_id=partner, device_id_type=MESH)
 
@@ -146,12 +141,7 @@
 
     own = own + dot(res, placed(feats, my_z))
 
-    loads("wd").wait()
-    for a in range(depth):
-        at = a % span * piece
-        wdd[a // span, :, at : at + piece] = vm["wd"][:, a, :]
-
-    pl.semaphore_wait(barrier, depth + experts - 1)
+    pl.semaphore_wait(barrier, 2 * hop + experts)
     exchange = to_partner(ex_src, ex_dst, 0)
     exchange.start()
 
@@ -208,17 +198,74 @@
         base = c * span * per
         for j in range(lane_groups):
             at = c * wide + j * LANES
-            block = chip[:, at : at + LANES].reshape(row_tiles, 8, LANES)
-            part[base + j * row_tiles : base + (j + 1) * row_tiles] = block.astype(BF16)
+            rows = chip[:, at : at + LANES].reshape(row_tiles, 8, LANES)
+            part[base + j * row_tiles : base + (j + 1) * row_tiles] = rows.astype(BF16)
         if span * per > tiles:
             part[base + tiles : base + span * per] = jnp.zeros((span * per - tiles, 8, LANES), BF16)
 
-    def rs_start(i, c):
-        peer = z_peer(i)
-        z_copy(0, part.at[pl.ds(peer * per, per)], rs_buf.at[i], peer).start()
-        return c
-
-    lax.fori_loop(0, depth - 1, rs_start, 0)
+    direct = 2 * hop - 1
+
+    def block(ref, z):
+        return ref.at[pl.ds(z * per, per)]
+
+    def rs_send(src, box, base, down):
+        up = depth - down
+        below = down <= 2 * hop
+        near = jnp.where(below, down < hop, up < hop)
+        step = jnp.where(below, -jnp.where(near, down, down - hop), jnp.where(near, up, up - hop))
+        length = jnp.abs(step) - 1
+        slot = jnp.where(
+            near,
+            direct + length + jnp.where(below, 0, hop - 1),
+            length + jnp.where(below, 0, hop),
+        )
+        group = base + jnp.where(near, 2, jnp.where(below, 0, 1))
+        pltpu.make_async_remote_copy(
+            src_ref=block(src, z_at(-down)), dst_ref=box.at[slot], send_sem=z_send.at[base],
+            recv_sem=z_recv.at[group], device_id=(my_dp, z_at(step), my_side), device_id_type=MESH,
+        ).start()
+
+    def rs_relay(src, box, out, base, side):
+        first_slot, count = ((0, hop), (hop, hop - 1))[side]
+        sign = (-1, 1)[side]
+        held = box.at[pl.ds(first_slot, count)]
+        z_wait(held, base + side).wait_recv()
+        total = src[pl.ds(z_at(sign * hop) * per, per)].astype(F32)
+        for n in range(count):
+            total = total + box[first_slot + n].astype(F32)
+        out[side] = total.astype(BF16)
+        pltpu.make_async_remote_copy(
+            src_ref=out.at[side], dst_ref=box.at[depth - 3 + side], send_sem=z_send.at[base],
+            recv_sem=z_recv.at[base + 2], device_id=(my_dp, z_at(sign * hop), my_side),
+            device_id_type=MESH,
+        ).start()
+
+    def z_wait(held, group, send=0):
+        return pltpu.make_async_remote_copy(
+            src_ref=held, dst_ref=held, send_sem=z_send.at[send], recv_sem=z_recv.at[group],
+            device_id=partner, device_id_type=MESH,
+        )
+
+    def rs_total(src, box, base):
+        z_wait(box.at[pl.ds(direct, 2 * hop)], base + 2).wait_recv()
+        total = src[pl.ds(my_z * per, per)].astype(F32)
+        for n in range(direct, depth - 1):
+            total = total + box[n].astype(F32)
+        z_wait(box, base, base).wait_send()
+        return total
+
+    downs = [n for d in range(hop, 0, -1) for n in (hop + d, depth - hop - d)]
+    downs += [n for d in range(hop - 1, 0, -1) for n in (d, depth - d)]
+    for down in dict.fromkeys(downs):
+        rs_send(part, inbox, 0, jnp.int32(down))
+
+    loads("wd").wait()
+    for a in range(depth):
+        at = a % span * piece
+        wdd[a // span, :, at : at + piece] = vm["wd"][:, a, :]
+
+    rs_relay(part, inbox, relay, 0, 0)
+    rs_relay(part, inbox, relay, 0, 1)
 
     kd = decay * k1
     kd_hi = kd.astype(BF16).astype(F32)
@@ -231,35 +278,38 @@
         )
         state_out[r, 0] = (decay2 * vm["state"][r, 0].astype(F32) + outer).astype(BF16)
 
-    z_copy(0, rs_buf, rs_buf, z_peer(0)).wait()
     mine = pl.ds(my_z * per, per)
-    total = part[mine].astype(F32)
-    for i in range(depth - 1):
-        total = total + rs_buf[i].astype(F32)
-    tsum[mine] = total.astype(BF16)
-
-    def ag_start(i, c):
-        peer = z_peer(i)
-        pltpu.make_async_remote_copy(
-            src_ref=tsum.at[mine], dst_ref=tsum.at[mine], send_sem=z_send.at[1],
-            recv_sem=z_recv.at[3 + my_chunk], device_id=(my_dp, peer, my_side), device_id_type=MESH,
-        ).start()
-        return c
-
-    lax.fori_loop(0, depth - 1, ag_start, 0)
-
-    for p, chunk in enumerate(order):
-        count = span * per if ahead[p] else (span - 1) * per
-        held = tsum.at[pl.ds(0, count)]
-        if count:
-            pltpu.make_async_remote_copy(
-                src_ref=held, dst_ref=held, send_sem=z_send.at[1], recv_sem=z_recv.at[3 + chunk],
-                device_id=partner, device_id_type=MESH,
-            ).wait_recv()
+    tsum[mine] = rs_total(part, inbox, 0).astype(BF16)
+
+    def ag_copy(origin, to):
+        held = block(tsum, origin)
+        return pltpu.make_async_remote_copy(
+            src_ref=held, dst_ref=held, send_sem=z_send.at[1], recv_sem=z_recv.at[6 + origin],
+            device_id=(my_dp, to, my_side), device_id_type=MESH,
+        )
+
+    for offset in range(hop, 0, -1):
+        for sign in (1, -1):
+            ag_copy(my_z, z_at(sign * offset)).start()
+    for sign, reach in ((1, hop), (-1, hop - 1)):
+        origin = z_at(-sign * hop)
+        ag_copy(origin, z_at(sign)).wait_recv()
+        for offset in range(reach, 0, -1):
+            ag_copy(origin, z_at(sign * offset)).start()
+
+    for p, chunk in enumerate(near_order):
+        for b in range(span):
+            origin = chunk * span + b
+            away = (origin - my_z + depth) % depth
+
+            def arrive(origin=origin):
+                ag_copy(origin, z_at(1)).wait_recv()
+
+            pl.when((away != 0) & (away != hop) & (away != depth - hop))(arrive)
         cols = []
         for j in range(lane_groups):
-            block = tsum[pl.ds(chunk * span * per + j * row_tiles, row_tiles)].astype(F32)
-            cols.append(block.reshape(tokens, LANES).astype(BF16))
+            rows = tsum[pl.ds(chunk * span * per + j * row_tiles, row_tiles)].astype(F32)
+            cols.append(rows.reshape(tokens, LANES).astype(BF16))
         last = jnp.zeros((main, LANES), F32)
         for j, col in enumerate(cols):
             disp[p, :, j] = dot(picks[0], col).reshape(experts, SLOTS, LANES).astype(BF16)
@@ -273,13 +323,13 @@
 
         lax.fori_loop(1, experts, go_start, 0)
         recv[p, 0] = disp[p, my_dp]
-        if not ahead[p]:
+        if not nearest[p]:
             resid_out[...] = lax.dot_general(
                 jnp.concatenate(cols, 1), placed(wide, my_z % span),
                 (((1,), (1,)), ((), ())), preferred_element_type=F32,
             ).astype(BF16)
 
-    z_copy(1, rs_buf, rs_buf, z_peer(0)).wait_send()
+    z_wait(inbox, 6, 1).wait_send()
     loads("wg").wait()
     loads("wu").wait()
     unpick = [
@@ -293,7 +343,7 @@
     gate_own = jnp.zeros((slots, hidden), F32)
     up_own = jnp.zeros((slots, hidden), F32)
     squares = jnp.zeros((slots, LANES), F32)
-    for p, chunk in enumerate(order):
+    for p, chunk in enumerate(near_order):
         dp_copy(p, disp.at[p, others], recv.at[p, others], dp_peer(1)).wait()
         last = recv[p, :, lane_groups].astype(F32).reshape(main, LANES).astype(BF16)
         xs = []
@@ -354,26 +404,28 @@
             lanes = [
                 mixed[t * 8 : t * 8 + 8, b * piece : (b + 1) * piece] for t in range(row_tiles)
             ]
-            pad = rs2_buf.shape[2] - row_tiles * piece
-            if pad:
-                lanes.append(jnp.zeros((8, pad), F32))
-            rs2_src[p, b] = jnp.concatenate(lanes, 1).astype(BF16)
+            if per * LANES > row_tiles * piece:
+                lanes.append(jnp.zeros((8, per * LANES - row_tiles * piece), F32))
+            packed = jnp.concatenate(lanes, 1)
+            dest = chunk * span + b
+            for t in range(per):
+                part2[dest * per + t] = packed[:, t * LANES : (t + 1) * LANES].astype(BF16)
         for b in range(span):
-            peer = chunk * span + b
-
-            def send(p=p, b=b, peer=peer):
-                z_copy(2, rs2_src.at[p, b], rs2_buf.at[my_z], peer).start()
-
-            if ahead[p]:
-                send()
-            else:
-                pl.when(peer != my_z)(send)
-    rs2_buf[my_z] = rs2_src[chunks - 1, my_z % span]
-    arrived = rs2_buf.at[pl.ds(0, depth - 1)]
-    z_copy(2, arrived, arrived, z_peer(0)).wait()
-    final = rs2_buf[0].astype(F32)
-    for i in range(1, depth):
-        final = final + rs2_buf[i].astype(F32)
+            down = (my_z - chunk * span - b + depth) % depth
+
+            def send(down=down):
+                rs_send(part2, inbox2, 3, down)
+
+            pl.when((down != 0) & (down != hop) & (down != depth - hop))(send)
+        if hop == span and ahead[p] == 1:
+            rs_relay(part2, inbox2, relay2, 3, 1)
+        if hop == span and ahead[p] == chunks - 1:
+            rs_relay(part2, inbox2, relay2, 3, 0)
+    if hop != span:
+        rs_relay(part2, inbox2, relay2, 3, 0)
+        rs_relay(part2, inbox2, relay2, 3, 1)
+    total = rs_total(part2, inbox2, 3)
+    final = jnp.concatenate([total[t] for t in range(per)], 1)
     for t in range(row_tiles):
         moe_out[t * 8 : t * 8 + 8, :] = final[:, t * piece : (t + 1) * piece].astype(BF16)
 
@@ -392,7 +444,6 @@
     wide = span * piece
     per = -(-(wide // LANES) * (tokens // 8) // span)
     slots = experts * SLOTS + experts
-    packed = -(-(tokens // 8) * piece // LANES) * LANES
     tiled = (chunks, experts, wide // LANES + 1, SLOTS, LANES)
     rows_y = 4 if experts == 16 else experts
     dims = (experts, depth, chunks, rows_y, requests, steps, top, piece, hidden, width)
@@ -410,6 +461,7 @@
         pltpu.VMEM((per * depth, 8, LANES), BF16),
         pltpu.VMEM((per * depth, 8, LANES), BF16),
         pltpu.VMEM((depth - 1, per, 8, LANES), BF16),
+        pltpu.VMEM((2, per, 8, LANES), BF16),
         pltpu.VMEM(tiled, BF16),
         pltpu.VMEM(tiled, BF16),
         pltpu.VMEM((chunks, 1, wide), F32),
@@ -419,13 +471,14 @@
         pltpu.VMEM((2, slots, hidden), BF16),
         pltpu.VMEM(tiled, BF16),
         pltpu.VMEM(tiled, BF16),
-        pltpu.VMEM((chunks, span, 8, packed), BF16),
-        pltpu.VMEM((depth, 8, packed), BF16),
+        pltpu.VMEM((per * depth, 8, LANES), BF16),
+        pltpu.VMEM((depth - 1, per, 8, LANES), BF16),
+        pltpu.VMEM((2, per, 8, LANES), BF16),
         dma((len(IN_NAMES),)),
         dma((3,)),
         dma((3,)),
-        dma((3,)),
-        dma((3 + chunks,)),
+        dma((4,)),
+        dma((6 + depth,)),
         dma((2 * chunks,)),
         dma((2 * chunks,)),
     ]

time: 65.8 us -> 66.7 us (1.014)
  Pallas kernels: 61.8 us -> 63 us
    pallas_call x1, Pallas kernels: 61.8 us -> 63 us  [layer(): pl.pallas_call(functools.partial(kernel, dims), out_shape=(pltpu.VMEM(sta...]
where the time goes in v3:
time: 66.7 us; the launch traced here: 65.8 us
  Pallas kernels  63 us (94%)
  local copies, waits for them, and re-layouts  1.5 us (2%)
  between operations  1.29 us (2%)
    pallas_call x1, Pallas kernels, layer(): pl.pallas_call(functools.partial(kernel, dims), out_shape=(pltpu.VMEM(sta...  63 us

profile of v3, /device:TPU:1, one launch (start us, length us, event | category | flops | bytes accessed | tf_op | source)
XLA Modules:
  0.0 65.8 jit_solution(505692646729478522)
XLA Ops:
  1.3 63.0 %layer.1 = (bf16[24,1,128,128]{3,2,1,0:T(8,128)(2,1)S(1)}, bf16[48,96]{1,0:T(8,128)(2,1)S(1)}, bf16[48,96]{1,0:T(8,128)(2,1)S(1)}) custom-call(bf16[24,2,128]{2,1,0:T(2,128)(2,1)} %refs_0_.1, bf16[24,2,128]{2,1,0:T(2,128)(2,1)} %refs_1_.1, bf16[24,2,128]{2,1,0:T(2,128)(2,1)} %refs_2_.1, f32[1,128]{1,0:T(1,128)} %bitcast.21, bf16[24,2,96]{2,1,0:T(2,128)(2,1)} %refs_4_.1, ...), custom_call_target="tpu_custom_call" | custom-call | tf_op jit(solution)/shard_map/layer/pallas_call | solution.py:486
  64.3 0.9 %copy.22 = bf16[24,1,128,128]{3,2,1,0:T(8,128)(2,1)} copy(bf16[24,1,128,128]{3,2,1,0:T(8,128)(2,1)S(1)} %get-tuple-element.11) | data formatting | bytes 1572864
  65.2 0.6 copy_bitcast_fusion

commit v4 on v3

--- a/solution.py
+++ b/solution.py
@@ -37,7 +37,7 @@
     vm = dict(zip(IN_NAMES, refs[n_in + 4 : 2 * n_in + 4]))
     (
         wdd, ex_src, ex_dst, part, tsum, inbox, relay, disp, recv, gain_v,
-        ss_src, ss_dst, gu_src, gu_dst, back, comb, part2, inbox2, relay2,
+        ss_src, ss_dst, gu_src, gu_dst, back, comb, part2, inbox2,
         in_sem, side_send, side_recv, z_send, z_recv, dp_send, dp_recv,
     ) = refs[2 * n_in + 4 :]
 
@@ -355,18 +355,23 @@
             xs.append((x * gain_v[chunk][:, j * LANES : (j + 1) * LANES]).astype(BF16))
         x = jnp.concatenate(xs, 1)
         rows = pl.ds(chunk * span, span)
+        final_chunk = p == chunks - 1
         gate_own = gate_own + dot(x, vm["wg"][rows].reshape(wide, hidden))
+        if final_chunk:
+            gu_src[0] = gate_own.astype(BF16)
+            gate_copy = to_partner(gu_src.at[0], gu_dst.at[0], 1)
+            gate_copy.start()
+            ss_src[...] = jnp.broadcast_to(jnp.sum(squares, 1, keepdims=True), (slots, LANES))
+            ss_copy = to_partner(ss_src, ss_dst, 2)
+            ss_copy.start()
         up_own = up_own + dot(x, vm["wu"][rows].reshape(wide, hidden))
-    gu_src[0] = gate_own.astype(BF16)
     gu_src[1] = up_own.astype(BF16)
-    ss_src[...] = jnp.broadcast_to(jnp.sum(squares, 1, keepdims=True), (slots, LANES))
-    gu_copy = to_partner(gu_src, gu_dst, 1)
-    ss_copy = to_partner(ss_src, ss_dst, 2)
-    gu_copy.start()
-    ss_copy.start()
+    up_copy = to_partner(gu_src.at[1], gu_dst.at[1], 3)
+    up_copy.start()
     ss_copy.wait()
     scale = lax.rsqrt((ss_src[...] + ss_dst[...]) / width + 1e-6)[:, :1]
-    gu_copy.wait()
+    gate_copy.wait()
+    up_copy.wait()
     gate_val = (gate_own + gu_dst[0].astype(F32)) * scale
     up_val = (up_own + gu_dst[1].astype(F32)) * scale
     act = (gate_val / (1.0 + jnp.exp(-gate_val)) * up_val).astype(BF16)
@@ -411,20 +416,23 @@
             for t in range(per):
                 part2[dest * per + t] = packed[:, t * LANES : (t + 1) * LANES].astype(BF16)
         for b in range(span):
-            down = (my_z - chunk * span - b + depth) % depth
-
-            def send(down=down):
-                rs_send(part2, inbox2, 3, down)
-
-            pl.when((down != 0) & (down != hop) & (down != depth - hop))(send)
-        if hop == span and ahead[p] == 1:
-            rs_relay(part2, inbox2, relay2, 3, 1)
-        if hop == span and ahead[p] == chunks - 1:
-            rs_relay(part2, inbox2, relay2, 3, 0)
-    if hop != span:
-        rs_relay(part2, inbox2, relay2, 3, 0)
-        rs_relay(part2, inbox2, relay2, 3, 1)
-    total = rs_total(part2, inbox2, 3)
+            peer = chunk * span + b
+
+            def send(peer=peer):
+                pltpu.make_async_remote_copy(
+                    src_ref=block(part2, peer), dst_ref=inbox2.at[my_z], send_sem=z_send.at[2],
+                    recv_sem=z_recv.at[3], device_id=(my_dp, peer, my_side), device_id_type=MESH,
+                ).start()
+
+            if ahead[p]:
+                send()
+            else:
+                pl.when(peer != my_z)(send)
+    inbox2[my_z] = part2[mine]
+    z_wait(inbox2.at[pl.ds(0, depth - 1)], 3, 2).wait()
+    total = inbox2[0].astype(F32)
+    for n in range(1, depth):
+        total = total + inbox2[n].astype(F32)
     final = jnp.concatenate([total[t] for t in range(per)], 1)
     for t in range(row_tiles):
         moe_out[t * 8 : t * 8 + 8, :] = final[:, t * piece : (t + 1) * piece].astype(BF16)
@@ -472,11 +480,10 @@
         pltpu.VMEM(tiled, BF16),
         pltpu.VMEM(tiled, BF16),
         pltpu.VMEM((per * depth, 8, LANES), BF16),
-        pltpu.VMEM((depth - 1, per, 8, LANES), BF16),
-        pltpu.VMEM((2, per, 8, LANES), BF16),
+        pltpu.VMEM((depth, per, 8, LANES), BF16),
         dma((len(IN_NAMES),)),
-        dma((3,)),
-        dma((3,)),
+        dma((4,)),
+        dma((4,)),
         dma((4,)),
         dma((6 + depth,)),
         dma((2 * chunks,)),

time: 66.7 us -> 64.4 us (0.966); the launches traced: 65.8 us -> 64.3 us
  Pallas kernels: 63 us -> 61.5 us
    pallas_call x1, Pallas kernels: 63 us -> 61.5 us  [layer(): pl.pallas_call(functools.partial(kernel, dims), out_shape=(pltpu.VMEM(sta...]
where the time goes in v4:
time: 64.4 us; the launch traced here: 64.3 us
  Pallas kernels  61.5 us (95%)
  local copies, waits for them, and re-layouts  1.5 us (2%)
  between operations  1.29 us (2%)
    pallas_call x1, Pallas kernels, layer(): pl.pallas_call(functools.partial(kernel, dims), out_shape=(pltpu.VMEM(sta...  61.5 us

profile of v4, /device:TPU:1, one launch (start us, length us, event | category | flops | bytes accessed | tf_op | source)
XLA Modules:
  0.0 64.3 jit_solution(17253601141867326954)
XLA Ops:
  1.3 61.5 %layer.1 = (bf16[24,1,128,128]{3,2,1,0:T(8,128)(2,1)S(1)}, bf16[48,96]{1,0:T(8,128)(2,1)S(1)}, bf16[48,96]{1,0:T(8,128)(2,1)S(1)}) custom-call(bf16[24,2,128]{2,1,0:T(2,128)(2,1)} %refs_0_.1, bf16[24,2,128]{2,1,0:T(2,128)(2,1)} %refs_1_.1, bf16[24,2,128]{2,1,0:T(2,128)(2,1)} %refs_2_.1, f32[1,128]{1,0:T(1,128)} %bitcast.21, bf16[24,2,96]{2,1,0:T(2,128)(2,1)} %refs_4_.1, ...), custom_call_target="tpu_custom_call" | custom-call | tf_op jit(solution)/shard_map/layer/pallas_call | solution.py:493
  62.7 0.9 %copy.22 = bf16[24,1,128,128]{3,2,1,0:T(8,128)(2,1)} copy(bf16[24,1,128,128]{3,2,1,0:T(8,128)(2,1)S(1)} %get-tuple-element.11) | data formatting | bytes 1572864
  63.6 0.6 copy_bitcast_fusion

commit v5 on v4

--- a/solution.py
+++ b/solution.py
@@ -12,7 +12,7 @@
 MESH = pl.DeviceIdType.MESH
 SLOTS = 8
 LANES = 128
-IN_NAMES = ("q", "k", "v", "hg", "res", "ng", "ids", "gates", "state", "wo", "wg", "wu", "wd")
+IN_NAMES = ("slope", "q", "k", "v", "hg", "res", "ng", "ids", "gates", "state", "wo", "wg", "wu", "wd")
 
 
 def dot(a, b):
@@ -33,13 +33,13 @@
     slots = main + experts
     n_in = len(IN_NAMES)
     hbm = dict(zip(IN_NAMES, refs[:n_in]))
-    slope_ref, state_out, resid_out, moe_out = refs[n_in : n_in + 4]
-    vm = dict(zip(IN_NAMES, refs[n_in + 4 : 2 * n_in + 4]))
+    state_out, resid_out, moe_out = refs[n_in : n_in + 3]
+    vm = dict(zip(IN_NAMES, refs[n_in + 3 : 2 * n_in + 3]))
     (
         wdd, ex_src, ex_dst, part, tsum, inbox, relay, disp, recv, gain_v,
-        ss_src, ss_dst, gu_src, gu_dst, back, comb, part2, inbox2,
+        gu_src, gu_dst, back, comb, part2, inbox2,
         in_sem, side_send, side_recv, z_send, z_recv, dp_send, dp_recv,
-    ) = refs[2 * n_in + 4 :]
+    ) = refs[2 * n_in + 3 :]
 
     my_dp = lax.axis_index("dp")
     my_z = lax.axis_index("heads")
@@ -62,6 +62,12 @@
         y = (my_dp % rows_y + i % rows_y) % rows_y
         return x * rows_y + y
 
+    def apart(i):
+        x, y = i // rows_y, i % rows_y
+        return min(x, columns - x) + min(y, rows_y - y)
+
+    dp_order = sorted(range(1, experts), key=apart, reverse=True)
+
     def home(i):
         x = (my_dp // rows_y - i // rows_y + columns) % columns
         y = (my_dp % rows_y - i % rows_y + rows_y) % rows_y
@@ -83,7 +89,7 @@
             device_id=(peer, my_z, my_side), device_id_type=MESH,
         )
 
-    for name in ("state", "q", "k", "v", "hg", "wo", "wd", "res", "ids", "gates", "ng", "wg", "wu"):
+    for name in ("state", "slope", "q", "k", "v", "hg", "wo", "wd", "res", "ids", "gates", "ng", "wg", "wu"):
         loads(name).start()
 
     barrier = pltpu.get_barrier_semaphore()
@@ -100,9 +106,9 @@
     lax.fori_loop(1, experts, greet_dp, 0)
     pl.semaphore_signal(barrier, 1, device_id=partner, device_id_type=MESH)
 
-    for name in ("q", "k", "v", "hg", "state"):
+    for name in ("slope", "q", "k", "v", "hg", "state"):
         loads(name).wait()
-    decay = jnp.exp(jnp.full((1, LANES), -slope_ref[0], F32))
+    decay = jnp.exp(-jnp.broadcast_to(vm["slope"][...], (1, LANES)))
     q = vm["q"][...].astype(F32)
     k = vm["k"][...].astype(F32)
     v = vm["v"][...].astype(F32)
@@ -139,11 +145,10 @@
         row = lax.broadcasted_iota(jnp.int32, (piece, size), 0)
         return (column == row + at * piece).astype(BF16)
 
-    own = own + dot(res, placed(feats, my_z))
-
     pl.semaphore_wait(barrier, 2 * hop + experts)
     exchange = to_partner(ex_src, ex_dst, 0)
     exchange.start()
+    own = own + dot(res, placed(feats, my_z))
 
     loads("ids").wait()
     loads("gates").wait()
@@ -316,12 +321,9 @@
             last = last + dot(picks[1 + j], col)
         disp[p, :, lane_groups] = last.reshape(experts, SLOTS, LANES).astype(BF16)
 
-        def go_start(i, c, p=p):
+        for i in dp_order:
             peer = dp_peer(i)
             dp_copy(p, disp.at[p, peer], recv.at[p, i], peer).start()
-            return c
-
-        lax.fori_loop(1, experts, go_start, 0)
         recv[p, 0] = disp[p, my_dp]
         if not nearest[p]:
             resid_out[...] = lax.dot_general(
@@ -358,22 +360,25 @@
         final_chunk = p == chunks - 1
         gate_own = gate_own + dot(x, vm["wg"][rows].reshape(wide, hidden))
         if final_chunk:
-            gu_src[0] = gate_own.astype(BF16)
+            spare = gu_src.shape[2] - hidden
+            squares = jnp.sum(squares, 1, keepdims=True)
+            high = squares.astype(BF16).astype(F32)
+            gu_src[0, :, :hidden] = gate_own.astype(BF16)
+            gu_src[0, :, hidden:] = jnp.broadcast_to(high, (slots, spare)).astype(BF16)
             gate_copy = to_partner(gu_src.at[0], gu_dst.at[0], 1)
             gate_copy.start()
-            ss_src[...] = jnp.broadcast_to(jnp.sum(squares, 1, keepdims=True), (slots, LANES))
-            ss_copy = to_partner(ss_src, ss_dst, 2)
-            ss_copy.start()
+            gu_src[1, :, hidden:] = jnp.broadcast_to(squares - high, (slots, spare)).astype(BF16)
         up_own = up_own + dot(x, vm["wu"][rows].reshape(wide, hidden))
-    gu_src[1] = up_own.astype(BF16)
-    up_copy = to_partner(gu_src.at[1], gu_dst.at[1], 3)
+    gu_src[1, :, :hidden] = up_own.astype(BF16)
+    up_copy = to_partner(gu_src.at[1], gu_dst.at[1], 2)
     up_copy.start()
-    ss_copy.wait()
-    scale = lax.rsqrt((ss_src[...] + ss_dst[...]) / width + 1e-6)[:, :1]
     gate_copy.wait()
     up_copy.wait()
-    gate_val = (gate_own + gu_dst[0].astype(F32)) * scale
-    up_val = (up_own + gu_dst[1].astype(F32)) * scale
+    for half in range(2):
+        squares = squares + gu_dst[half, :, hidden : hidden + 1].astype(F32)
+    scale = lax.rsqrt(squares / width + 1e-6)
+    gate_val = (gate_own + gu_dst[0, :, :hidden].astype(F32)) * scale
+    up_val = (up_own + gu_dst[1, :, :hidden].astype(F32)) * scale
     act = (gate_val / (1.0 + jnp.exp(-gate_val)) * up_val).astype(BF16)
 
     for p, chunk in enumerate(order):
@@ -388,11 +393,8 @@
             )
         back[p, :, lane_groups] = last.reshape(experts, SLOTS, LANES).astype(BF16)
 
-        def back_start(i, c, p=p):
+        for i in dp_order:
             dp_copy(chunks + p, back.at[p, i], comb.at[p, my_dp], home(i)).start()
-            return c
-
-        lax.fori_loop(1, experts, back_start, 0)
         comb[p, my_dp] = back[p, 0]
 
     for p, chunk in enumerate(order):
@@ -456,7 +458,7 @@
     rows_y = 4 if experts == 16 else experts
     dims = (experts, depth, chunks, rows_y, requests, steps, top, piece, hidden, width)
     operands = {
-        "q": q, "k": k, "v": v, "hg": hg.reshape(1, head), "res": res, "ng": ng.reshape(1, width),
+        "slope": slopes.reshape(1, 1), "q": q, "k": k, "v": v, "hg": hg.reshape(1, head), "res": res, "ng": ng.reshape(1, width),
         "ids": ids.transpose(1, 2, 0), "gates": gates.transpose(1, 2, 0), "state": state, "wo": wo,
         "wg": wg[0], "wu": wu[0], "wd": wd[0],
     }
@@ -473,18 +475,16 @@
         pltpu.VMEM(tiled, BF16),
         pltpu.VMEM(tiled, BF16),
         pltpu.VMEM((chunks, 1, wide), F32),
-        pltpu.VMEM((slots, LANES), F32),
-        pltpu.VMEM((slots, LANES), F32),
-        pltpu.VMEM((2, slots, hidden), BF16),
-        pltpu.VMEM((2, slots, hidden), BF16),
+        pltpu.VMEM((2, slots, (hidden // LANES + 1) * LANES), BF16),
+        pltpu.VMEM((2, slots, (hidden // LANES + 1) * LANES), BF16),
         pltpu.VMEM(tiled, BF16),
         pltpu.VMEM(tiled, BF16),
         pltpu.VMEM((per * depth, 8, LANES), BF16),
         pltpu.VMEM((depth, per, 8, LANES), BF16),
         dma((len(IN_NAMES),)),
-        dma((4,)),
-        dma((4,)),
-        dma((4,)),
+        dma((3,)),
+        dma((3,)),
+        dma((3,)),
         dma((6 + depth,)),
         dma((2 * chunks,)),
         dma((2 * chunks,)),
@@ -497,7 +497,7 @@
             pltpu.VMEM((tokens, piece), BF16),
             pltpu.VMEM((tokens, piece), BF16),
         ),
-        in_specs=[any_spec] * len(arrays) + [pl.BlockSpec(memory_space=pltpu.SMEM)],
+        in_specs=[any_spec] * len(arrays),
         out_specs=(
             pl.BlockSpec(memory_space=pltpu.VMEM),
             pl.BlockSpec(memory_space=pltpu.VMEM),
@@ -508,7 +508,7 @@
             collective_id=0, has_side_effects=True, vmem_limit_bytes=56 * 1024 * 1024
         ),
         name="layer",
-    )(*arrays, slopes)
+    )(*arrays)
     back = lambda x: x.reshape(steps, requests, piece).transpose(1, 0, 2)
     return state_new, back(resid), back(moe)
 

time: 64.4 us -> 63.5 us (0.986)
  Pallas kernels: 61.5 us -> 60.5 us
    pallas_call x1, Pallas kernels: 61.5 us -> 60.5 us  [layer(): pl.pallas_call(functools.partial(kernel, dims), out_shape=(pltpu.VMEM(sta...]
where the time goes in v5:
time: 63.5 us; the launch traced here: 63.3 us
  Pallas kernels  60.5 us (95%)
  local copies, waits for them, and re-layouts  1.5 us (2%)
  between operations  1.29 us (2%)
    pallas_call x1, Pallas kernels, layer(): pl.pallas_call(functools.partial(kernel, dims), out_shape=(pltpu.VMEM(sta...  60.5 us

profile of v5, /device:TPU:1, one launch (start us, length us, event | category | flops | bytes accessed | tf_op | source)
XLA Modules:
  0.0 63.3 jit_solution(2115591547196440428)
XLA Ops:
  1.3 60.5 %layer.1 = (bf16[24,1,128,128]{3,2,1,0:T(8,128)(2,1)S(1)}, bf16[48,96]{1,0:T(8,128)(2,1)S(1)}, bf16[48,96]{1,0:T(8,128)(2,1)S(1)}) custom-call(f32[1,1]{1,0:T(1,128)} %bitcast.14.refs_0_, bf16[24,2,128]{2,1,0:T(2,128)(2,1)} %refs_1_.1, bf16[24,2,128]{2,1,0:T(2,128)(2,1)} %refs_2_.1, bf16[24,2,128]{2,1,0:T(2,128)(2,1)} %refs_3_.1, f32[1,128]{1,0:T(1,128)} %bitcast.23, ...), custom_call_target="tpu_custom_call" | custom-call | tf_op jit(solution)/shard_map/layer/pallas_call | solution.py:493
  61.8 0.9 %copy.22 = bf16[24,1,128,128]{3,2,1,0:T(8,128)(2,1)} copy(bf16[24,1,128,128]{3,2,1,0:T(8,128)(2,1)S(1)} %get-tuple-element.11) | data formatting | bytes 1572864
  62.7 0.6 copy_bitcast_fusion

commit v6 on v5

--- a/solution.py
+++ b/solution.py
@@ -264,13 +264,13 @@
     for down in dict.fromkeys(downs):
         rs_send(part, inbox, 0, jnp.int32(down))
 
+    rs_relay(part, inbox, relay, 0, 0)
+    rs_relay(part, inbox, relay, 0, 1)
+
     loads("wd").wait()
     for a in range(depth):
         at = a % span * piece
         wdd[a // span, :, at : at + piece] = vm["wd"][:, a, :]
-
-    rs_relay(part, inbox, relay, 0, 0)
-    rs_relay(part, inbox, relay, 0, 1)
 
     kd = decay * k1
     kd_hi = kd.astype(BF16).astype(F32)

time: 63.5 us -> 63 us (level)
  no operation moved by 1% of the time
where the time goes in v6:
time: 63 us; the launch traced here: 62.9 us
  Pallas kernels  60.1 us (95%)
  local copies, waits for them, and re-layouts  1.5 us (2%)
  between operations  1.29 us (2%)
    pallas_call x1, Pallas kernels, layer(): pl.pallas_call(functools.partial(kernel, dims), out_shape=(pltpu.VMEM(sta...  60.1 us

profile of v6, /device:TPU:1, one launch (start us, length us, event | category | flops | bytes accessed | tf_op | source)
XLA Modules:
  0.0 62.9 jit_solution(16076594921293523677)
XLA Ops:
  1.3 60.1 %layer.1 = (bf16[24,1,128,128]{3,2,1,0:T(8,128)(2,1)S(1)}, bf16[48,96]{1,0:T(8,128)(2,1)S(1)}, bf16[48,96]{1,0:T(8,128)(2,1)S(1)}) custom-call(f32[1,1]{1,0:T(1,128)} %bitcast.14.refs_0_, bf16[24,2,128]{2,1,0:T(2,128)(2,1)} %refs_1_.1, bf16[24,2,128]{2,1,0:T(2,128)(2,1)} %refs_2_.1, bf16[24,2,128]{2,1,0:T(2,128)(2,1)} %refs_3_.1, f32[1,128]{1,0:T(1,128)} %bitcast.23, ...), custom_call_target="tpu_custom_call" | custom-call | tf_op jit(solution)/shard_map/layer/pallas_call | solution.py:493
  61.4 0.9 %copy.22 = bf16[24,1,128,128]{3,2,1,0:T(8,128)(2,1)} copy(bf16[24,1,128,128]{3,2,1,0:T(8,128)(2,1)S(1)} %get-tuple-element.11) | data formatting | bytes 1572864
  62.3 0.6 copy_bitcast_fusion
